TPU v7x, 32 devices: a whole 2x2x4 slice. The times are simulated.
32 devices in a mesh: ctx: 8 (over z, x), wsh: 4 (over y, core).
Axes of the slice: x: 2, y: 2, z: 4, core: 2. Of those that a mesh axis runs over, the one named last changes fastest.
Arguments:
- inputs: bfloat16 [8, 1024, 768], P('wsh', 'ctx'), may hold values from -6 to 6
- teacher: bfloat16 [8, 1024, 768], P('wsh', 'ctx'), may hold values from -6 to 6
- seq_lengths: int32 [8], P('wsh'), may hold values from 256 to 1024, as said below
- gain_attn: bfloat16 [768], P('wsh'), may hold values from 0.5 to 1.5
- w_query: bfloat16 [768, 768], P('wsh'), may hold values from -0.109375 to 0.109375
- w_key: bfloat16 [768, 768], P('wsh'), may hold values from -0.109375 to 0.109375
- w_value: bfloat16 [768, 768], P('wsh'), may hold values from -0.21875 to 0.21875
- w_out: bfloat16 [768, 768], P('wsh'), may hold values from -2.5 to 2.5
- bias_table: bfloat16 [32, 12], P('wsh'), may hold values from -4 to 4
- gain_ffn: bfloat16 [768], P('wsh'), may hold values from 0.5 to 1.5
- w_inner: bfloat16 [768, 3072], P('wsh'), may hold values from -0.21875 to 0.21875
- w_outer: bfloat16 [3072, 768], P('wsh'), may hold values from -0.109375 to 0.109375
Outputs:
- layer_out: bfloat16 [8, 1024, 768], P('wsh', 'ctx')
- loss_value: float32 [], replicated
- input_grad: float32 [8, 1024, 768], P('wsh', 'ctx')
- gain_attn_grad: float32 [768], P('wsh')
- w_query_grad: float32 [768, 768], P('wsh')
- w_key_grad: float32 [768, 768], P('wsh')
- w_value_grad: float32 [768, 768], P('wsh')
- w_out_grad: float32 [768, 768], P('wsh')
- bias_table_grad: float32 [32, 12], P('wsh')
- gain_ffn_grad: float32 [768], P('wsh')
- w_inner_grad: float32 [768, 3072], P('wsh')
- w_outer_grad: float32 [3072, 768], P('wsh')
Inputs may be any that keep to these rules, and one draw needn't show every extreme that they name: `seq_lengths`: in each aligned group of 2 sequences exactly one, chosen by the seed, has all 1024 tokens valid; every other sequence has fewer.
All inputs are finite; a program needn't handle non-finite values.
Results may differ from a plain program's by a relative error of at most 0.017.
Values may be sent and summed in bfloat16 or wider, within the bound.
No kernel may reach another device: no remote copies, remote signals or barrier semaphores. Data moves between devices by JAX's collectives and lax.ppermute only.
A program may use at most 128 MiB of HBM per device.

v0:
```python
import jax
import jax.numpy as jnp
from jax import lax
from jax.sharding import PartitionSpec as P

D = 768
H = 12
DH = 64
BUCKETS = 32
SEQ_DEV = 2
PIECE = 128
EPS = 1e-06
NEG_FILL = -1e30
BUCKET_EDGES = (12, 16, 23, 32, 46, 64, 91)


def passed_along(block, axis, distance):
    devices = range(lax.axis_size(axis))
    route = [((i - distance) % len(devices), i) for i in devices]
    return lax.ppermute(block, axis, route)


def for_sending(value):

    def short(part):
        return part.astype(jnp.bfloat16) if part.dtype == jnp.float32 else part

    return jax.tree.map(short, value)


def bucket_index(offset):
    distance = jnp.abs(offset)
    far_bucket = 8 + sum(((distance >= edge).astype(jnp.int32) for edge in BUCKET_EDGES))
    near_or_far = jnp.where(distance < 8, distance, far_bucket)
    return near_or_far + jnp.where(offset > 0, 16, 0)


def rms_scale(values, gain_vector):
    return values * lax.rsqrt(jnp.mean(values * values, axis=-1, keepdims=True) + EPS) * gain_vector


def gelu_exact(values):
    return jax.nn.gelu(values, approximate=False)


def rows_product(left, right):
    return lax.dot_general(
        left, right, (((0,), (0,)), ((), ())), preferred_element_type=jnp.float32
    )


def times_transposed(left, right):
    return lax.dot_general(
        left, right, (((1,), (1,)), ((), ())), preferred_element_type=jnp.float32
    )


def move_keys(blocks):
    return (passed_along(blocks[0], "ctx", 1),)


def move_grads(blocks):
    return (passed_along(for_sending(blocks[0]), "ctx", 1),)


def on_device(
    inputs,
    teacher,
    seq_lengths,
    gain_attn,
    w_query,
    w_key,
    w_value,
    w_out,
    bias_table,
    gain_ffn,
    w_inner,
    w_outer,
):
    cycle_size = lax.axis_size("ctx")
    cycle_pos = lax.axis_index("ctx")
    token_total = SEQ_DEV * PIECE * cycle_size * lax.axis_size("wsh")
    row_count = SEQ_DEV * PIECE
    shards = (gain_attn, w_query, w_key, w_value, w_out, bias_table, gain_ffn, w_inner, w_outer)
    gathered = (
        lax.all_gather(shards[0], "wsh", axis=0, tiled=True),
        lax.all_gather(shards[1], "wsh", axis=0, tiled=True),
        lax.all_gather(shards[2], "wsh", axis=0, tiled=True),
        lax.all_gather(shards[3], "wsh", axis=0, tiled=True),
        lax.all_gather(shards[4], "wsh", axis=0, tiled=True),
        lax.all_gather(shards[5], "wsh", axis=0, tiled=True),
        lax.all_gather(shards[6], "wsh", axis=0, tiled=True),
        lax.all_gather(shards[7], "wsh", axis=0, tiled=True),
        lax.all_gather(shards[8], "wsh", axis=0, tiled=True),
    )
    (
        attn_gain,
        query_full,
        key_full,
        value_full,
        out_full,
        table_full,
        ffn_gain,
        inner_full,
        outer_full,
    ) = gathered
    lane_plans = ((0, H, 1),)
    x_rows = inputs.reshape(row_count, D).astype(jnp.float32)
    normed, attn_norm_back = jax.vjp(rms_scale, x_rows, attn_gain.astype(jnp.float32))
    normed_low = normed.astype(jnp.bfloat16)
    query_low = jnp.dot(normed_low, query_full, preferred_element_type=jnp.float32).astype(
        jnp.bfloat16
    )
    key_low = jnp.dot(normed_low, key_full, preferred_element_type=jnp.float32).astype(jnp.bfloat16)
    value_low = jnp.dot(normed_low, value_full, preferred_element_type=jnp.float32).astype(
        jnp.bfloat16
    )
    query_heads = query_low.reshape(SEQ_DEV, PIECE, H, DH)
    key_value = jnp.stack([key_low, value_low]).reshape(2, SEQ_DEV, PIECE, H * DH)
    places = jnp.arange(PIECE, dtype=jnp.int32)
    query_places = cycle_pos * PIECE + places
    bucket_ids = jnp.arange(BUCKETS, dtype=jnp.int32)

    def lane_blocks(stacked):
        return tuple((stacked for plan in lane_plans))

    def lane_scores(lane_plan, query_part, lane_block, key_start, table_rows):
        head_count = lane_plan[1] - lane_plan[0]
        key_count = lane_block.shape[2]
        key_places = key_start + jnp.arange(key_count, dtype=jnp.int32)
        offset = (key_places[None, :] - query_places[:, None]).reshape(-1)
        onehot = (bucket_index(offset)[None, :] == bucket_ids[:, None]).astype(jnp.bfloat16)
        bias_rows = jnp.dot(table_rows, onehot, preferred_element_type=jnp.float32)
        key_part = lane_block[0].reshape(SEQ_DEV, key_count, head_count, DH)
        scores = jnp.einsum(
            "sihd,sjhd->shij", query_part, key_part, preferred_element_type=jnp.float32
        )
        scores = scores + bias_rows.reshape(head_count, PIECE, key_count)[None]
        key_ok = key_places[None, :] < seq_lengths[:, None]
        return (jnp.where(key_ok[:, None, None, :], scores, NEG_FILL), onehot)

    table_forward = table_full.T

    def absorb(lane_plan, lane_state, lane_block, key_start):
        head_count = lane_plan[1] - lane_plan[0]
        key_count = lane_block.shape[2]
        row_max, row_total, accum = lane_state
        scores, onehot = lane_scores(lane_plan, query_heads, lane_block, key_start, table_forward)
        new_max = jnp.maximum(row_max, jnp.max(scores, axis=-1))
        rescale = jnp.exp(row_max - new_max)
        weights = jnp.exp(scores - new_max[..., None])
        row_total = row_total * rescale + jnp.sum(weights, axis=-1)
        value_part = lane_block[1].reshape(SEQ_DEV, key_count, head_count, DH)
        update = jnp.einsum(
            "shij,sjhd->sihd",
            weights.astype(jnp.bfloat16),
            value_part,
            preferred_element_type=jnp.float32,
        )
        accum = accum * jnp.transpose(rescale, (0, 2, 1))[..., None] + update
        return (new_max, row_total, accum)

    def empty_state(plan):
        head_count = plan[1] - plan[0]
        return (
            jnp.full((SEQ_DEV, head_count, PIECE), NEG_FILL, jnp.float32),
            jnp.zeros((SEQ_DEV, head_count, PIECE), jnp.float32),
            jnp.zeros((SEQ_DEV, PIECE, head_count, DH), jnp.float32),
        )

    def empty_accum(plan):
        head_count = plan[1] - plan[0]
        return (
            jnp.zeros((SEQ_DEV, PIECE, head_count, DH), jnp.float32),
            jnp.zeros((head_count, BUCKETS), jnp.float32),
        )

    blocks = lane_blocks(key_value)
    states = tuple(
        (
            absorb(plan, empty_state(plan), lane_block, cycle_pos * PIECE)
            for plan, lane_block in zip(lane_plans, blocks)
        )
    )

    def forward_turn(turn_index, loop_carry):
        arrived = move_keys(loop_carry[0])
        new_states = tuple(
            (
                absorb(
                    plan,
                    lane_state,
                    lane_block,
                    (cycle_pos - plan[2] * turn_index) % cycle_size * PIECE,
                )
                for plan, lane_state, lane_block in zip(lane_plans, loop_carry[1], arrived)
            )
        )
        return (arrived, new_states)

    blocks, states = lax.fori_loop(1, cycle_size, forward_turn, (blocks, states))
    log_totals = jnp.concatenate(
        [lane_state[0] + jnp.log(lane_state[1]) for lane_state in states], axis=1
    )
    attn_out = jnp.concatenate(
        [
            lane_state[2] / jnp.transpose(lane_state[1], (0, 2, 1))[..., None]
            for lane_state in states
        ],
        axis=2,
    )
    attn_low = attn_out.reshape(row_count, H * DH).astype(jnp.bfloat16)
    hidden = x_rows + jnp.dot(attn_low, out_full, preferred_element_type=jnp.float32)
    normed_ffn, ffn_norm_back = jax.vjp(rms_scale, hidden, ffn_gain.astype(jnp.float32))
    ffn_low = normed_ffn.astype(jnp.bfloat16)
    inner_sum = jnp.dot(ffn_low, inner_full, preferred_element_type=jnp.float32)
    active, gelu_back = jax.vjp(gelu_exact, inner_sum)
    active_low = active.astype(jnp.bfloat16)
    result = hidden + jnp.dot(active_low, outer_full, preferred_element_type=jnp.float32)
    row_valid = (
        (query_places[None, :] < seq_lengths[:, None]).astype(jnp.float32).reshape(row_count, 1)
    )
    deviation = result - teacher.reshape(row_count, D).astype(jnp.float32)
    square_sum, valid_count = lax.psum(
        (jnp.sum(deviation * deviation * row_valid), jnp.sum(row_valid)), ("ctx", "wsh")
    )
    loss_value = square_sum / (valid_count * D)
    result_grad = token_total / valid_count * deviation * row_valid
    result_low = result_grad.astype(jnp.bfloat16)
    query_back = gathered[1]
    key_back = gathered[2]
    value_back = gathered[3]
    out_back = gathered[4]
    table_back = gathered[5].T
    inner_back = gathered[7]
    outer_back = gathered[8]
    outer_grad = rows_product(active_low, result_low)
    active_grad = times_transposed(result_low, outer_back)
    inner_grad = gelu_back(active_grad)[0].astype(jnp.bfloat16)
    inner_wgrad = rows_product(ffn_low, inner_grad)
    ffn_normed_grad = times_transposed(inner_grad, inner_back)
    hidden_part, ffn_gain_grad = ffn_norm_back(ffn_normed_grad)
    hidden_grad = result_grad + hidden_part
    hidden_low = hidden_grad.astype(jnp.bfloat16)
    out_wgrad = rows_product(attn_low, hidden_low)
    dout_heads = (
        times_transposed(hidden_low, out_back).astype(jnp.bfloat16).reshape(SEQ_DEV, PIECE, H, DH)
    )
    out_dot = jnp.transpose(jnp.sum(dout_heads.astype(jnp.float32) * attn_out, axis=-1), (0, 2, 1))

    def lane_back(lane_plan, lane_block, lane_accum, key_start):
        low_head, high_head = (lane_plan[0], lane_plan[1])
        head_count = high_head - low_head
        key_count = lane_block.shape[2]
        scores, onehot = lane_scores(lane_plan, query_heads, lane_block, key_start, table_back)
        probability = jnp.exp(scores - log_totals[:, low_head:high_head, :, None])
        prob_low = probability.astype(jnp.bfloat16)
        key_part = lane_block[0].reshape(SEQ_DEV, key_count, head_count, DH)
        value_part = lane_block[1].reshape(SEQ_DEV, key_count, head_count, DH)
        value_grad = jnp.einsum(
            "shij,sihd->sjhd", prob_low, dout_heads, preferred_element_type=jnp.float32
        )
        prob_grad = jnp.einsum(
            "sihd,sjhd->shij", dout_heads, value_part, preferred_element_type=jnp.float32
        )
        score_grad = (probability * (prob_grad - out_dot[:, low_head:high_head, :, None])).astype(
            jnp.bfloat16
        )
        query_grad = lane_accum[0] + jnp.einsum(
            "shij,sjhd->sihd", score_grad, key_part, preferred_element_type=jnp.float32
        )
        key_grad = jnp.einsum(
            "shij,sihd->sjhd", score_grad, query_heads, preferred_element_type=jnp.float32
        )
        table_grad = lane_accum[1] + jnp.einsum(
            "shk,bk->hb",
            score_grad.reshape(SEQ_DEV, head_count, PIECE * key_count),
            onehot,
            preferred_element_type=jnp.float32,
        )
        term = jnp.stack([key_grad, value_grad]).reshape(2, SEQ_DEV, key_count, head_count * DH)
        return (term, (query_grad, table_grad))

    blocks = lane_blocks(key_value)
    outcome = [
        lane_back(plan, lane_block, empty_accum(plan), cycle_pos * PIECE)
        for plan, lane_block in zip(lane_plans, blocks)
    ]
    grad_blocks = move_grads(tuple((entry[0] for entry in outcome)))
    accums = tuple((entry[1] for entry in outcome))

    def back_turn(turn_index, loop_carry):
        arrived = move_keys(loop_carry[0])
        outcome = [
            lane_back(
                plan,
                lane_block,
                lane_accum,
                (cycle_pos - plan[2] * turn_index) % cycle_size * PIECE,
            )
            for plan, lane_block, lane_accum in zip(lane_plans, arrived, loop_carry[2])
        ]
        new_grads = move_grads(
            tuple((grad_block + entry[0] for grad_block, entry in zip(loop_carry[1], outcome)))
        )
        return (arrived, new_grads, tuple((entry[1] for entry in outcome)))

    blocks, grad_blocks, accums = lax.fori_loop(
        1, cycle_size, back_turn, (blocks, grad_blocks, accums)
    )
    pair_grads = grad_blocks[0]
    query_grad_low = (
        jnp.concatenate([lane_accum[0] for lane_accum in accums], axis=2)
        .reshape(row_count, H * DH)
        .astype(jnp.bfloat16)
    )
    key_grad_low = pair_grads[0].reshape(row_count, H * DH).astype(jnp.bfloat16)
    value_grad_low = pair_grads[1].reshape(row_count, H * DH).astype(jnp.bfloat16)
    table_grad = jnp.concatenate([lane_accum[1] for lane_accum in accums], axis=0).T
    query_wgrad = rows_product(normed_low, query_grad_low)
    key_wgrad = rows_product(normed_low, key_grad_low)
    value_wgrad = rows_product(normed_low, value_grad_low)
    normed_grad = (
        times_transposed(query_grad_low, query_back)
        + times_transposed(key_grad_low, key_back)
        + times_transposed(value_grad_low, value_back)
    )
    input_part, attn_gain_grad = attn_norm_back(normed_grad)
    input_grad = hidden_grad + input_part
    local_grads = (
        attn_gain_grad,
        query_wgrad,
        key_wgrad,
        value_wgrad,
        out_wgrad,
        table_grad,
        ffn_gain_grad,
        inner_wgrad,
        outer_grad,
    )
    shares = (
        lax.psum_scatter(
            local_grads[0].astype(jnp.bfloat16), "wsh", scatter_dimension=0, tiled=True
        ).astype(jnp.float32),
        lax.psum_scatter(
            local_grads[1].astype(jnp.bfloat16), "wsh", scatter_dimension=0, tiled=True
        ).astype(jnp.float32),
        lax.psum_scatter(
            local_grads[2].astype(jnp.bfloat16), "wsh", scatter_dimension=0, tiled=True
        ).astype(jnp.float32),
        lax.psum_scatter(
            local_grads[3].astype(jnp.bfloat16), "wsh", scatter_dimension=0, tiled=True
        ).astype(jnp.float32),
        lax.psum_scatter(
            local_grads[4].astype(jnp.bfloat16), "wsh", scatter_dimension=0, tiled=True
        ).astype(jnp.float32),
        lax.psum_scatter(
            local_grads[5].astype(jnp.bfloat16), "wsh", scatter_dimension=0, tiled=True
        ).astype(jnp.float32),
        lax.psum_scatter(
            local_grads[6].astype(jnp.bfloat16), "wsh", scatter_dimension=0, tiled=True
        ).astype(jnp.float32),
        lax.psum_scatter(
            local_grads[7].astype(jnp.bfloat16), "wsh", scatter_dimension=0, tiled=True
        ).astype(jnp.float32),
        lax.psum_scatter(
            local_grads[8].astype(jnp.bfloat16), "wsh", scatter_dimension=0, tiled=True
        ).astype(jnp.float32),
    )
    totals = lax.psum(
        (
            shares[0],
            shares[1],
            shares[2],
            shares[3],
            shares[4],
            shares[5],
            shares[6],
            shares[7],
            shares[8],
        ),
        "ctx",
    )
    return (
        result.reshape(SEQ_DEV, PIECE, D).astype(jnp.bfloat16),
        loss_value,
        input_grad.reshape(SEQ_DEV, PIECE, D),
        totals[0],
        totals[1],
        totals[2],
        totals[3],
        totals[4],
        totals[5],
        totals[6],
        totals[7],
        totals[8],
    )


def solution(mesh):
    placed = (
        P("wsh", "ctx", None),
        P("wsh", "ctx", None),
        P("wsh"),
        P("wsh"),
        P("wsh", None),
        P("wsh", None),
        P("wsh", None),
        P("wsh", None),
        P("wsh", None),
        P("wsh"),
        P("wsh", None),
        P("wsh", None),
    )
    return jax.shard_map(
        on_device,
        mesh=mesh,
        in_specs=placed,
        out_specs=(
            P("wsh", "ctx", None),
            P(),
            P("wsh", "ctx", None),
            P("wsh"),
            P("wsh", None),
            P("wsh", None),
            P("wsh", None),
            P("wsh", None),
            P("wsh", None),
            P("wsh"),
            P("wsh", None),
            P("wsh", None),
        ),
        check_vma=False,
    )
```

profile of v0, /device:TPU:0, one launch (start us, length us, event | category | flops | bytes accessed | tf_op | source)
XLA Modules:
  0.0 1081.6 jit_solution(2276786720739246816)
XLA Ops:
  13.8 8.4 all-reduce.8
  22.3 5.2 all_gather.31
  28.3 1.1 copy.159
  33.1 1.7 convolution_convert_fusion.9
  35.1 14.0 %all-gather.7.cloned.1.call-done = bf16[768,768]{1,0:T(8,128)(2,1)} async-done(((bf16[192,768]{1,0:T(8,128)(2,1)}), bf16[768,768]{1,0:T(8,128)(2,1)}) %all-gather.7.cloned.1.call-update) | async-done | bytes 1179664 | tf_op jit(solution)/shard_map/all_gather | solution.py:88
  49.1 1.7 convolution_convert_fusion.11
  51.2 1.7 fusion.112
  54.1 14.0 %all-gather.9.cloned.1.call-done = bf16[768,768]{1,0:T(8,128)(2,1)} async-done(((bf16[192,768]{1,0:T(8,128)(2,1)}), bf16[768,768]{1,0:T(8,128)(2,1)}) %all-gather.9.cloned.1.call-update) | async-done | bytes 1179664 | tf_op jit(solution)/shard_map/all_gather | solution.py:89
  68.1 1.7 convolution_convert_fusion.10
  72.0 155.8 %while.44 = (s32[]{:T(128)}, bf16[2,2,128,768]{2,3,1,0:T(8,128)(2,1)}, f32[2,12,128]{2,1,0:T(8,128)S(1)}, f32[2,12,128]{2,1,0:T(8,128)}, f32[2,128,12,64]{1,3,2,...) while((s32[]{:T(128)}, ...), condition=%wide.region_6.7_spmd.clone, body=%wide.region_3.6_spmd.clone.sunk | while | flops 117384720 | bytes 21013696 | solution.py:201
  72.5 1.5 collective-permute-start
  75.9 19.2 %collective-permute-done = bf16[2,2,128,768]{2,3,1,0:T(8,128)(2,1)S(1)} collective-permute-done((bf16[2,2,128,768]{2,3,1,0:T(8,128)(2,1)}, bf16[2,2,128,768]{2,3,1,0:T(8,128)(2,1)S(1)}, u32[]{:S(2)}, u32[]{:S(2)}) %collective-permute-start) | collective-permute-done | bytes 786464 | tf_op jit(solution)/shard_map/while/body/eval_jaxpr/ppermute | solution.py:20
  99.3 19.9 %collective-permute-done = bf16[2,2,128,768]{2,3,1,0:T(8,128)(2,1)S(1)} collective-permute-done((bf16[2,2,128,768]{2,3,1,0:T(8,128)(2,1)}, bf16[2,2,128,768]{2,3,1,0:T(8,128)(2,1)S(1)}, u32[]{:S(2)}, u32[]{:S(2)}) %collective-permute-start) | collective-permute-done | bytes 786464 | tf_op jit(solution)/shard_map/while/body/eval_jaxpr/ppermute | solution.py:20
  123.3 18.9 %collective-permute-done = bf16[2,2,128,768]{2,3,1,0:T(8,128)(2,1)S(1)} collective-permute-done((bf16[2,2,128,768]{2,3,1,0:T(8,128)(2,1)}, bf16[2,2,128,768]{2,3,1,0:T(8,128)(2,1)S(1)}, u32[]{:S(2)}, u32[]{:S(2)}) %collective-permute-start) | collective-permute-done | bytes 786464 | tf_op jit(solution)/shard_map/while/body/eval_jaxpr/ppermute | solution.py:20
  146.5 18.0 %collective-permute-done = bf16[2,2,128,768]{2,3,1,0:T(8,128)(2,1)S(1)} collective-permute-done((bf16[2,2,128,768]{2,3,1,0:T(8,128)(2,1)}, bf16[2,2,128,768]{2,3,1,0:T(8,128)(2,1)S(1)}, u32[]{:S(2)}, u32[]{:S(2)}) %collective-permute-start) | collective-permute-done | bytes 786464 | tf_op jit(solution)/shard_map/while/body/eval_jaxpr/ppermute | solution.py:20
  168.6 17.1 %collective-permute-done = bf16[2,2,128,768]{2,3,1,0:T(8,128)(2,1)S(1)} collective-permute-done((bf16[2,2,128,768]{2,3,1,0:T(8,128)(2,1)}, bf16[2,2,128,768]{2,3,1,0:T(8,128)(2,1)S(1)}, u32[]{:S(2)}, u32[]{:S(2)}) %collective-permute-start) | collective-permute-done | bytes 786464 | tf_op jit(solution)/shard_map/while/body/eval_jaxpr/ppermute | solution.py:20
  189.9 16.2 %collective-permute-done = bf16[2,2,128,768]{2,3,1,0:T(8,128)(2,1)S(1)} collective-permute-done((bf16[2,2,128,768]{2,3,1,0:T(8,128)(2,1)}, bf16[2,2,128,768]{2,3,1,0:T(8,128)(2,1)S(1)}, u32[]{:S(2)}, u32[]{:S(2)}) %collective-permute-start) | collective-permute-done | bytes 786464 | tf_op jit(solution)/shard_map/while/body/eval_jaxpr/ppermute | solution.py:20
  210.3 15.2 %collective-permute-done = bf16[2,2,128,768]{2,3,1,0:T(8,128)(2,1)S(1)} collective-permute-done((bf16[2,2,128,768]{2,3,1,0:T(8,128)(2,1)}, bf16[2,2,128,768]{2,3,1,0:T(8,128)(2,1)S(1)}, u32[]{:S(2)}, u32[]{:S(2)}) %collective-permute-start) | collective-permute-done | bytes 786464 | tf_op jit(solution)/shard_map/while/body/eval_jaxpr/ppermute | solution.py:20
  228.5 1.7 fusion.106
  230.2 2.1 multiply_reduce_fusion.4
  233.1 11.2 %multiply_convert_fusion.1 = (bf16[256,3072]{1,0:T(8,128)(2,1)S(1)}, f32[256,3072]{1,0:T(8,128)}, f32[256,3072]{1,0:T(8,128)}) fusion(bf16[768,3072]{1,0:T(8,128)(2,1)} %all-gather.15.cloned.1.call-done, f32[256,768]{1,0:T(8,128)S(1)} %get-tuple-element.884, f32[768]{0:T(1024)S(1)} %copy-done.42, f32[256]{0:T(256)S(1)} %fusion.98), kind=kOutput, calls=%fused_computation.67 | convolution fusion | flops 1259667456 | bytes 13373440 | tf_op jit(solution)/shard_map/dot_general | solution.py:216
  244.3 5.0 multiply_reduce_fusion.3
  249.3 37.3 %all-reduce.5 = (f32[]{:T(128)}, f32[]{:T(128)}) all-reduce(f32[]{:T(128)} %get-tuple-element.886, f32[]{:T(128)} %get-tuple-element.855), channel_id=1, replica_groups=mesh['ctx'=8,'wsh'=4] {'ctx','wsh'}, use_global_device_ids=true, to_apply=%region_9.10 | all-reduce | flops 2 | bytes 16 | tf_op jit(solution)/shard_map/psum | solution.py:224
  287.3 1.3 fusion.71
  288.6 6.4 add_convert_fusion
  295.1 2.1 multiply_reduce_fusion
  297.3 2.5 fusion.57
  302.4 1.6 multiply_reduce_fusion.1
  304.8 1.4 convert_reduce_fusion.1
  307.9 2.3 collective-permute-start.3
  310.2 1.5 convolution_convert_fusion.2
  311.8 1.3 copy.178
  314.9 14.6 %collective-permute-done.3 = bf16[2,2,128,768]{2,3,1,0:T(8,128)(2,1)S(1)} collective-permute-done((bf16[2,2,128,768]{2,3,1,0:T(8,128)(2,1)}, bf16[2,2,128,768]{2,3,1,0:T(8,128)(2,1)S(1)}, u32[]{:S(2)}, u32[]{:S(2)}) %collective-permute-start.3) | collective-permute-done | bytes 786464 | tf_op jit(solution)/shard_map/ppermute | solution.py:20
  329.5 279.1 %while.45 = (s32[]{:T(128)}, bf16[2,2,128,768]{2,3,1,0:T(8,128)(2,1)}, bf16[2,2,128,768]{2,3,1,0:T(8,128)(2,1)S(1)}, f32[2,128,12,64]{1,3,2,0:T(8,128)S(1)}, f32...) while((s32[]{:T(128)}, ...), condition=%wide.region_17.18_spmd.clone, body=%wide.region_15.17_spmd.clone.sunk | while | flops 283444096 | bytes 33844516 | solution.py:308
  330.0 1.1 fusion.219
  331.4 19.0 %collective-permute-done.1 = bf16[2,2,128,768]{2,3,1,0:T(8,128)(2,1)S(1)} collective-permute-done((bf16[2,2,128,768]{2,3,1,0:T(8,128)(2,1)}, bf16[2,2,128,768]{2,3,1,0:T(8,128)(2,1)S(1)}, u32[]{:S(2)}, u32[]{:S(2)}) %collective-permute-start.1) | collective-permute-done | bytes 786464 | tf_op jit(solution)/shard_map/while/body/eval_jaxpr/ppermute | solution.py:20
  355.4 17.0 %collective-permute-done.2 = bf16[2,2,128,768]{2,3,1,0:T(8,128)(2,1)S(1)} collective-permute-done((bf16[2,2,128,768]{2,3,1,0:T(8,128)(2,1)S(1)}, bf16[2,2,128,768]{2,3,1,0:T(8,128)(2,1)S(1)}, u32[]{:S(2)}, u32[]{:S(2)}) %collective-permute-start.2) | collective-permute-done | bytes 786464 | tf_op jit(solution)/shard_map/while/body/eval_jaxpr/ppermute | solution.py:20
  372.6 1.1 fusion.219
  374.1 17.2 %collective-permute-done.1 = bf16[2,2,128,768]{2,3,1,0:T(8,128)(2,1)S(1)} collective-permute-done((bf16[2,2,128,768]{2,3,1,0:T(8,128)(2,1)}, bf16[2,2,128,768]{2,3,1,0:T(8,128)(2,1)S(1)}, u32[]{:S(2)}, u32[]{:S(2)}) %collective-permute-start.1) | collective-permute-done | bytes 786464 | tf_op jit(solution)/shard_map/while/body/eval_jaxpr/ppermute | solution.py:20
  396.2 15.2 %collective-permute-done.2 = bf16[2,2,128,768]{2,3,1,0:T(8,128)(2,1)S(1)} collective-permute-done((bf16[2,2,128,768]{2,3,1,0:T(8,128)(2,1)S(1)}, bf16[2,2,128,768]{2,3,1,0:T(8,128)(2,1)S(1)}, u32[]{:S(2)}, u32[]{:S(2)}) %collective-permute-start.2) | collective-permute-done | bytes 786464 | tf_op jit(solution)/shard_map/while/body/eval_jaxpr/ppermute | solution.py:20
  411.6 1.1 fusion.219
  413.1 15.3 %collective-permute-done.1 = bf16[2,2,128,768]{2,3,1,0:T(8,128)(2,1)S(1)} collective-permute-done((bf16[2,2,128,768]{2,3,1,0:T(8,128)(2,1)}, bf16[2,2,128,768]{2,3,1,0:T(8,128)(2,1)S(1)}, u32[]{:S(2)}, u32[]{:S(2)}) %collective-permute-start.1) | collective-permute-done | bytes 786464 | tf_op jit(solution)/shard_map/while/body/eval_jaxpr/ppermute | solution.py:20
  433.4 15.0 %collective-permute-done.2 = bf16[2,2,128,768]{2,3,1,0:T(8,128)(2,1)S(1)} collective-permute-done((bf16[2,2,128,768]{2,3,1,0:T(8,128)(2,1)S(1)}, bf16[2,2,128,768]{2,3,1,0:T(8,128)(2,1)S(1)}, u32[]{:S(2)}, u32[]{:S(2)}) %collective-permute-start.2) | collective-permute-done | bytes 786464 | tf_op jit(solution)/shard_map/while/body/eval_jaxpr/ppermute | solution.py:20
  450.0 13.8 %collective-permute-done.1 = bf16[2,2,128,768]{2,3,1,0:T(8,128)(2,1)S(1)} collective-permute-done((bf16[2,2,128,768]{2,3,1,0:T(8,128)(2,1)}, bf16[2,2,128,768]{2,3,1,0:T(8,128)(2,1)S(1)}, u32[]{:S(2)}, u32[]{:S(2)}) %collective-permute-start.1) | collective-permute-done | bytes 786464 | tf_op jit(solution)/shard_map/while/body/eval_jaxpr/ppermute | solution.py:20
  468.8 15.8 %collective-permute-done.2 = bf16[2,2,128,768]{2,3,1,0:T(8,128)(2,1)S(1)} collective-permute-done((bf16[2,2,128,768]{2,3,1,0:T(8,128)(2,1)S(1)}, bf16[2,2,128,768]{2,3,1,0:T(8,128)(2,1)S(1)}, u32[]{:S(2)}, u32[]{:S(2)}) %collective-permute-start.2) | collective-permute-done | bytes 786464 | tf_op jit(solution)/shard_map/while/body/eval_jaxpr/ppermute | solution.py:20
  486.3 15.6 %collective-permute-done.1 = bf16[2,2,128,768]{2,3,1,0:T(8,128)(2,1)S(1)} collective-permute-done((bf16[2,2,128,768]{2,3,1,0:T(8,128)(2,1)}, bf16[2,2,128,768]{2,3,1,0:T(8,128)(2,1)S(1)}, u32[]{:S(2)}, u32[]{:S(2)}) %collective-permute-start.1) | collective-permute-done | bytes 786464 | tf_op jit(solution)/shard_map/while/body/eval_jaxpr/ppermute | solution.py:20
  506.9 18.0 %collective-permute-done.2 = bf16[2,2,128,768]{2,3,1,0:T(8,128)(2,1)S(1)} collective-permute-done((bf16[2,2,128,768]{2,3,1,0:T(8,128)(2,1)S(1)}, bf16[2,2,128,768]{2,3,1,0:T(8,128)(2,1)S(1)}, u32[]{:S(2)}, u32[]{:S(2)}) %collective-permute-start.2) | collective-permute-done | bytes 786464 | tf_op jit(solution)/shard_map/while/body/eval_jaxpr/ppermute | solution.py:20
  526.5 17.8 %collective-permute-done.1 = bf16[2,2,128,768]{2,3,1,0:T(8,128)(2,1)S(1)} collective-permute-done((bf16[2,2,128,768]{2,3,1,0:T(8,128)(2,1)}, bf16[2,2,128,768]{2,3,1,0:T(8,128)(2,1)S(1)}, u32[]{:S(2)}, u32[]{:S(2)}) %collective-permute-start.1) | collective-permute-done | bytes 786464 | tf_op jit(solution)/shard_map/while/body/eval_jaxpr/ppermute | solution.py:20
  549.3 20.3 %collective-permute-done.2 = bf16[2,2,128,768]{2,3,1,0:T(8,128)(2,1)S(1)} collective-permute-done((bf16[2,2,128,768]{2,3,1,0:T(8,128)(2,1)S(1)}, bf16[2,2,128,768]{2,3,1,0:T(8,128)(2,1)S(1)}, u32[]{:S(2)}, u32[]{:S(2)}) %collective-permute-start.2) | collective-permute-done | bytes 786464 | tf_op jit(solution)/shard_map/while/body/eval_jaxpr/ppermute | solution.py:20
  571.3 20.1 %collective-permute-done.1 = bf16[2,2,128,768]{2,3,1,0:T(8,128)(2,1)S(1)} collective-permute-done((bf16[2,2,128,768]{2,3,1,0:T(8,128)(2,1)}, bf16[2,2,128,768]{2,3,1,0:T(8,128)(2,1)S(1)}, u32[]{:S(2)}, u32[]{:S(2)}) %collective-permute-start.1) | collective-permute-done | bytes 786464 | tf_op jit(solution)/shard_map/while/body/eval_jaxpr/ppermute | solution.py:20
  596.4 12.2 %collective-permute-done.2 = bf16[2,2,128,768]{2,3,1,0:T(8,128)(2,1)S(1)} collective-permute-done((bf16[2,2,128,768]{2,3,1,0:T(8,128)(2,1)S(1)}, bf16[2,2,128,768]{2,3,1,0:T(8,128)(2,1)S(1)}, u32[]{:S(2)}, u32[]{:S(2)}) %collective-permute-start.2) | collective-permute-done | bytes 786464 | tf_op jit(solution)/shard_map/while/body/eval_jaxpr/ppermute | solution.py:20
  609.6 1.6 convolution_convert_fusion.4
  611.3 1.6 convolution_convert_fusion.3
  613.4 1.5 convolution_convert_fusion.5
  615.1 5.2 convolution_convert_fusion.1
  620.4 1.3 copy-done.20
  621.7 3.6 convolution_convert_fusion
  628.9 1.5 convolution_add_fusion.1
  631.2 11.3 %all-reduce.7 = (bf16[768]{0:T(1024)(128)(2,1)S(1)}, bf16[32,12]{1,0:T(8,128)(2,1)S(1)}, bf16[768]{0:T(1024)(128)(2,1)S(1)}) all-reduce(bf16[768]{0:T(1024)(128)(2,1)S(1)} %get-tuple-element.789, bf16[32,12]{1,0:T(8,128)(2,1)S(1)} %copy.186, bf16[768]{0:T(1024)(128)(2,1)S(1)} %copy-done.64), channel_id=2, replica_groups=mesh['ctx'=8,'wsh'=4] {'wsh'}, use_global_device_ids=true, to_apply=%region_20.21.clone | all-reduce | flops 1920 | bytes 7680
  643.6 21.0 %reduce-scatter.11.cloned.1.call-done = bf16[192,768]{1,0:T(8,128)(2,1)} async-done(((bf16[768,768]{1,0:T(8,128)(2,1)}), bf16[192,768]{1,0:T(8,128)(2,1)}) %reduce-scatter.11.cloned.1.call-update) | async-done | bytes 294928 | tf_op jit(solution)/shard_map/reduce_scatter | solution.py:351
  664.7 28.9 %reduce-scatter.7.cloned.1.call-done = bf16[192,768]{1,0:T(8,128)(2,1)} async-done(((bf16[768,768]{1,0:T(8,128)(2,1)}), bf16[192,768]{1,0:T(8,128)(2,1)}) %reduce-scatter.7.cloned.1.call-update) | async-done | bytes 294928 | tf_op jit(solution)/shard_map/reduce_scatter | solution.py:345
  693.6 50.4 %reduce-scatter.15.cloned.1.call-done = bf16[192,3072]{1,0:T(8,128)(2,1)} async-done(((bf16[768,3072]{1,0:T(8,128)(2,1)}), bf16[192,3072]{1,0:T(8,128)(2,1)}) %reduce-scatter.15.cloned.1.call-update) | async-done | bytes 1179664 | tf_op jit(solution)/shard_map/reduce_scatter | solution.py:363
  744.0 50.4 %reduce-scatter.17.cloned.1.call-done = bf16[768,768]{1,0:T(8,128)(2,1)} async-done(((bf16[3072,768]{1,0:T(8,128)(2,1)}), bf16[768,768]{1,0:T(8,128)(2,1)}) %reduce-scatter.17.cloned.1.call-update) | async-done | bytes 1179664 | tf_op jit(solution)/shard_map/reduce_scatter | solution.py:366
  794.4 279.1 %all-reduce.10 = (f32[192]{0:T(256)}, f32[192,768]{1,0:T(8,128)}, f32[192,768]{1,0:T(8,128)}, f32[192,768]{1,0:T(8,128)}, f32[192,768]{1,0:T(8,128)}, /*index=5*...) all-reduce(f32[192]{0:T(256)S(1)} %get-tuple-element.893, ...), channel_id=1, replica_groups=mesh['ctx'=8,'wsh'=4] {'ctx'}, use_global_device_ids=true, to_apply=%region_21.22 | all-reduce | flops 1769952 | bytes 10620672 | tf_op jit(solution)/shard_map/psum | solution.py:370
  (572 shorter events, 97.5 us)
Async XLA Ops:
  7.2 4.8 copy-start.63
  7.2 6.1 copy-start.67
  7.2 6.3 copy-start.68
  7.2 15.1 %copy-start.62 = (bf16[8,12]{1,0:T(8,128)(2,1)S(1)}, bf16[8,12]{1,0:T(8,128)(2,1)}, u32[]{:S(2)}) copy-start(bf16[8,12]{1,0:T(8,128)(2,1)} %param.24) | copy-start | bytes 580
  7.2 25.8 %all-gather.11.cloned.1.call-start = ((), (), s32[]{:S(2)}) async-start(), calls=%async_computation.8 | async-start | bytes 1474560 | tf_op jit(solution)/shard_map/all_gather | solution.py:87
  8.0 41.1 %all-gather.7.cloned.1.call-start = ((), (), s32[]{:S(2)}) async-start(), calls=%async_computation.6 | async-start | bytes 1474560 | tf_op jit(solution)/shard_map/all_gather | solution.py:88
  8.7 59.4 %all-gather.9.cloned.1.call-start = ((), (), s32[]{:S(2)}) async-start(), calls=%async_computation.7 | async-start | bytes 1474560 | tf_op jit(solution)/shard_map/all_gather | solution.py:89
  9.5 220.8 %all-gather.13.cloned.1.call-start = ((), (), s32[]{:S(2)}) async-start(), calls=%async_computation.9 | async-start | bytes 1474560 | tf_op jit(solution)/shard_map/all_gather | solution.py:90
  10.0 223.0 %all-gather.15.cloned.1.call-start = ((), (), s32[]{:S(2)}) async-start(), calls=%async_computation.10 | async-start | bytes 5898240 | tf_op jit(solution)/shard_map/all_gather | solution.py:93
  10.6 233.7 %all-gather.17.cloned.1.call-start = ((), (), s32[]{:S(2)}) async-start(), calls=%async_computation.11 | async-start | bytes 5898240 | tf_op jit(solution)/shard_map/all_gather | solution.py:94
  11.2 632.4 %reduce-scatter.13.cloned.1.call-start = ((), (), s32[]{:S(2)}) async-start(), calls=%async_computation.15 | async-start | bytes 1474560 | tf_op jit(solution)/shard_map/reduce_scatter | solution.py:354
  11.9 20.0 %copy-start.49 = (f32[256]{0:T(256)}, f32[256]{0:T(256)S(1)}, u32[]{:S(2)}) copy-start(f32[256]{0:T(256)S(1)} %bitcast_rsqrt_fusion) | copy-start | bytes 3076
  22.1 10.0 copy-start.45
  22.3 5.7 copy-start.40
  35.1 17.8 %copy-start.8 = (bf16[2,128,12,64]{1,0,3,2:T(2,128)(2,1)}, bf16[2,128,12,64]{1,0,3,2:T(2,128)(2,1)S(1)}, u32[]{:S(2)}) copy-start(bf16[2,128,12,64]{1,0,3,2:T(2,128)(2,1)S(1)} %reshape.466) | copy-start | bytes 1179652
  52.9 18.7 %copy-start = (f32[2,12,128,128]{2,3,1,0:T(8,128)}, f32[2,12,128,128]{2,3,1,0:T(8,128)S(1)}, u32[]{:S(2)}) copy-start(f32[2,12,128,128]{2,3,1,0:T(8,128)S(1)} %get-tuple-element.882) | copy-start | bytes 4718596
  72.5 22.6 %collective-permute-start = (bf16[2,2,128,768]{2,3,1,0:T(8,128)(2,1)}, bf16[2,2,128,768]{2,3,1,0:T(8,128)(2,1)S(1)}, u32[]{:S(2)}, u32[]{:S(2)}) collective-permute-start(bf16[2,2,128,768]{2,3,1,0:T(8,128)(2,1)} %get-tuple-element.1078), channel_id=1, source_target_pairs={{28,0},{0,4},{4,8},{8,12},{12,16},{16,20},{20,24},{24,28},{29,1},{... | collective-permute-start | bytes 2359304 | tf_op jit(solution)/shard_map/while/body/eval_jaxpr/ppermute | solution.py:20
  97.4 21.8 %collective-permute-start = (bf16[2,2,128,768]{2,3,1,0:T(8,128)(2,1)}, bf16[2,2,128,768]{2,3,1,0:T(8,128)(2,1)S(1)}, u32[]{:S(2)}, u32[]{:S(2)}) collective-permute-start(bf16[2,2,128,768]{2,3,1,0:T(8,128)(2,1)} %get-tuple-element.1078), channel_id=1, source_target_pairs={{28,0},{0,4},{4,8},{8,12},{12,16},{16,20},{20,24},{24,28},{29,1},{... | collective-permute-start | bytes 2359304 | tf_op jit(solution)/shard_map/while/body/eval_jaxpr/ppermute | solution.py:20
  121.4 20.8 %collective-permute-start = (bf16[2,2,128,768]{2,3,1,0:T(8,128)(2,1)}, bf16[2,2,128,768]{2,3,1,0:T(8,128)(2,1)S(1)}, u32[]{:S(2)}, u32[]{:S(2)}) collective-permute-start(bf16[2,2,128,768]{2,3,1,0:T(8,128)(2,1)} %get-tuple-element.1078), channel_id=1, source_target_pairs={{28,0},{0,4},{4,8},{8,12},{12,16},{16,20},{20,24},{24,28},{29,1},{... | collective-permute-start | bytes 2359304 | tf_op jit(solution)/shard_map/while/body/eval_jaxpr/ppermute | solution.py:20
  144.5 19.9 %collective-permute-start = (bf16[2,2,128,768]{2,3,1,0:T(8,128)(2,1)}, bf16[2,2,128,768]{2,3,1,0:T(8,128)(2,1)S(1)}, u32[]{:S(2)}, u32[]{:S(2)}) collective-permute-start(bf16[2,2,128,768]{2,3,1,0:T(8,128)(2,1)} %get-tuple-element.1078), channel_id=1, source_target_pairs={{28,0},{0,4},{4,8},{8,12},{12,16},{16,20},{20,24},{24,28},{29,1},{... | collective-permute-start | bytes 2359304 | tf_op jit(solution)/shard_map/while/body/eval_jaxpr/ppermute | solution.py:20
  166.7 19.0 %collective-permute-start = (bf16[2,2,128,768]{2,3,1,0:T(8,128)(2,1)}, bf16[2,2,128,768]{2,3,1,0:T(8,128)(2,1)S(1)}, u32[]{:S(2)}, u32[]{:S(2)}) collective-permute-start(bf16[2,2,128,768]{2,3,1,0:T(8,128)(2,1)} %get-tuple-element.1078), channel_id=1, source_target_pairs={{28,0},{0,4},{4,8},{8,12},{12,16},{16,20},{20,24},{24,28},{29,1},{... | collective-permute-start | bytes 2359304 | tf_op jit(solution)/shard_map/while/body/eval_jaxpr/ppermute | solution.py:20
  188.0 18.1 %collective-permute-start = (bf16[2,2,128,768]{2,3,1,0:T(8,128)(2,1)}, bf16[2,2,128,768]{2,3,1,0:T(8,128)(2,1)S(1)}, u32[]{:S(2)}, u32[]{:S(2)}) collective-permute-start(bf16[2,2,128,768]{2,3,1,0:T(8,128)(2,1)} %get-tuple-element.1078), channel_id=1, source_target_pairs={{28,0},{0,4},{4,8},{8,12},{12,16},{16,20},{20,24},{24,28},{29,1},{... | collective-permute-start | bytes 2359304 | tf_op jit(solution)/shard_map/while/body/eval_jaxpr/ppermute | solution.py:20
  208.3 17.2 %collective-permute-start = (bf16[2,2,128,768]{2,3,1,0:T(8,128)(2,1)}, bf16[2,2,128,768]{2,3,1,0:T(8,128)(2,1)S(1)}, u32[]{:S(2)}, u32[]{:S(2)}) collective-permute-start(bf16[2,2,128,768]{2,3,1,0:T(8,128)(2,1)} %get-tuple-element.1078), channel_id=1, source_target_pairs={{28,0},{0,4},{4,8},{8,12},{12,16},{16,20},{20,24},{24,28},{29,1},{... | collective-permute-start | bytes 2359304 | tf_op jit(solution)/shard_map/while/body/eval_jaxpr/ppermute | solution.py:20
  232.3 12.0 %copy-start.60 = (f32[256]{0:T(256)}, f32[256]{0:T(256)S(1)}, u32[]{:S(2)}) copy-start(f32[256]{0:T(256)S(1)} %get-tuple-element.883) | copy-start | bytes 3076
  232.3 64.9 %copy-start.14 = (f32[256,768]{1,0:T(8,128)}, f32[256,768]{1,0:T(8,128)S(1)}, u32[]{:S(2)}) copy-start(f32[256,768]{1,0:T(8,128)S(1)} %get-tuple-element.884) | copy-start | bytes 2359300
  232.3 11.9 %copy-start.51 = (f32[256]{0:T(256)}, f32[256]{0:T(256)S(1)}, u32[]{:S(2)}) copy-start(f32[256]{0:T(256)S(1)} %fusion.98) | copy-start | bytes 3076
  233.1 11.2 %copy-start.59 = (f32[256]{0:T(256)S(1)}, f32[256]{0:T(256)}, u32[]{:S(2)}) copy-start(f32[256]{0:T(256)} %convert_bitcast_fusion.1) | copy-start | bytes 3076
  244.2 5.1 copy-start.19
  249.3 45.7 %copy-start.23 = (f32[256,768]{1,0:T(8,128)}, f32[256,768]{1,0:T(8,128)S(1)}, u32[]{:S(2)}) copy-start(f32[256,768]{1,0:T(8,128)S(1)} %get-tuple-element.887) | copy-start | bytes 2359300
  287.3 7.8 slice-start
  288.6 6.5 copy-start.25
  288.6 6.5 copy-start.43
  288.6 6.5 copy-start.52
  288.6 6.5 slice-start.1
  299.8 10.4 copy-start.2
  307.9 21.6 %collective-permute-start.3 = (bf16[2,2,128,768]{2,3,1,0:T(8,128)(2,1)}, bf16[2,2,128,768]{2,3,1,0:T(8,128)(2,1)S(1)}, u32[]{:S(2)}, u32[]{:S(2)}) collective-permute-start(bf16[2,2,128,768]{2,3,1,0:T(8,128)(2,1)} %pad_maximum_fusion.1), channel_id=1, source_target_pairs={{28,0},{0,4},{4,8},{8,12},{12,16},{16,20},{20,24},{24,28},{29,1},{... | collective-permute-start | bytes 2359304 | tf_op jit(solution)/shard_map/ppermute | solution.py:20
  311.8 331.9 %reduce-scatter.9.cloned.1.call-start = ((), (), s32[]{:S(2)}) async-start(), calls=%async_computation.13 | async-start | bytes 1474560 | tf_op jit(solution)/shard_map/reduce_scatter | solution.py:348
  329.7 20.7 %collective-permute-start.1 = (bf16[2,2,128,768]{2,3,1,0:T(8,128)(2,1)}, bf16[2,2,128,768]{2,3,1,0:T(8,128)(2,1)S(1)}, u32[]{:S(2)}, u32[]{:S(2)}) collective-permute-start(bf16[2,2,128,768]{2,3,1,0:T(8,128)(2,1)} %get-tuple-element.1127), channel_id=1, source_target_pairs={{28,0},{0,4},{4,8},{8,12},{12,16},{16,20},{20,24},{24,28},{29,1},{... | collective-permute-start | bytes 2359304 | tf_op jit(solution)/shard_map/while/body/eval_jaxpr/ppermute | solution.py:20
  352.9 19.6 %collective-permute-start.2 = (bf16[2,2,128,768]{2,3,1,0:T(8,128)(2,1)S(1)}, bf16[2,2,128,768]{2,3,1,0:T(8,128)(2,1)S(1)}, u32[]{:S(2)}, u32[]{:S(2)}) collective-permute-start(bf16[2,2,128,768]{2,3,1,0:T(8,128)(2,1)S(1)} %fusion.222), channel_id=1, source_target_pairs={{28,0},{0,4},{4,8},{8,12},{12,16},{16,20},{20,24},{24,28},{29,1},{... | collective-permute-start | bytes 2359304 | tf_op jit(solution)/shard_map/while/body/eval_jaxpr/ppermute | solution.py:20
  354.7 17.7 %copy-start.57 = (f32[12,32]{1,0:T(8,128)}, f32[12,32]{1,0:T(8,128)S(1)}, u32[]{:S(2)}) copy-start(f32[12,32]{1,0:T(8,128)S(1)} %fusion.224) | copy-start | bytes 4612 | tf_op jit(solution)/shard_map/while
  372.4 18.8 %collective-permute-start.1 = (bf16[2,2,128,768]{2,3,1,0:T(8,128)(2,1)}, bf16[2,2,128,768]{2,3,1,0:T(8,128)(2,1)S(1)}, u32[]{:S(2)}, u32[]{:S(2)}) collective-permute-start(bf16[2,2,128,768]{2,3,1,0:T(8,128)(2,1)} %get-tuple-element.1127), channel_id=1, source_target_pairs={{28,0},{0,4},{4,8},{8,12},{12,16},{16,20},{20,24},{24,28},{29,1},{... | collective-permute-start | bytes 2359304 | tf_op jit(solution)/shard_map/while/body/eval_jaxpr/ppermute | solution.py:20
  393.7 17.7 %collective-permute-start.2 = (bf16[2,2,128,768]{2,3,1,0:T(8,128)(2,1)S(1)}, bf16[2,2,128,768]{2,3,1,0:T(8,128)(2,1)S(1)}, u32[]{:S(2)}, u32[]{:S(2)}) collective-permute-start(bf16[2,2,128,768]{2,3,1,0:T(8,128)(2,1)S(1)} %fusion.222), channel_id=1, source_target_pairs={{28,0},{0,4},{4,8},{8,12},{12,16},{16,20},{20,24},{24,28},{29,1},{... | collective-permute-start | bytes 2359304 | tf_op jit(solution)/shard_map/while/body/eval_jaxpr/ppermute | solution.py:20
  395.6 15.8 %copy-start.57 = (f32[12,32]{1,0:T(8,128)}, f32[12,32]{1,0:T(8,128)S(1)}, u32[]{:S(2)}) copy-start(f32[12,32]{1,0:T(8,128)S(1)} %fusion.224) | copy-start | bytes 4612 | tf_op jit(solution)/shard_map/while
  411.4 16.9 %collective-permute-start.1 = (bf16[2,2,128,768]{2,3,1,0:T(8,128)(2,1)}, bf16[2,2,128,768]{2,3,1,0:T(8,128)(2,1)S(1)}, u32[]{:S(2)}, u32[]{:S(2)}) collective-permute-start(bf16[2,2,128,768]{2,3,1,0:T(8,128)(2,1)} %get-tuple-element.1127), channel_id=1, source_target_pairs={{28,0},{0,4},{4,8},{8,12},{12,16},{16,20},{20,24},{24,28},{29,1},{... | collective-permute-start | bytes 2359304 | tf_op jit(solution)/shard_map/while/body/eval_jaxpr/ppermute | solution.py:20
  430.8 17.5 %collective-permute-start.2 = (bf16[2,2,128,768]{2,3,1,0:T(8,128)(2,1)S(1)}, bf16[2,2,128,768]{2,3,1,0:T(8,128)(2,1)S(1)}, u32[]{:S(2)}, u32[]{:S(2)}) collective-permute-start(bf16[2,2,128,768]{2,3,1,0:T(8,128)(2,1)S(1)} %fusion.222), channel_id=1, source_target_pairs={{28,0},{0,4},{4,8},{8,12},{12,16},{16,20},{20,24},{24,28},{29,1},{... | collective-permute-start | bytes 2359304 | tf_op jit(solution)/shard_map/while/body/eval_jaxpr/ppermute | solution.py:20
  432.7 15.7 %copy-start.57 = (f32[12,32]{1,0:T(8,128)}, f32[12,32]{1,0:T(8,128)S(1)}, u32[]{:S(2)}) copy-start(f32[12,32]{1,0:T(8,128)S(1)} %fusion.224) | copy-start | bytes 4612 | tf_op jit(solution)/shard_map/while
  448.4 15.4 %collective-permute-start.1 = (bf16[2,2,128,768]{2,3,1,0:T(8,128)(2,1)}, bf16[2,2,128,768]{2,3,1,0:T(8,128)(2,1)S(1)}, u32[]{:S(2)}, u32[]{:S(2)}) collective-permute-start(bf16[2,2,128,768]{2,3,1,0:T(8,128)(2,1)} %get-tuple-element.1127), channel_id=1, source_target_pairs={{28,0},{0,4},{4,8},{8,12},{12,16},{16,20},{20,24},{24,28},{29,1},{... | collective-permute-start | bytes 2359304 | tf_op jit(solution)/shard_map/while/body/eval_jaxpr/ppermute | solution.py:20
  466.3 18.4 %collective-permute-start.2 = (bf16[2,2,128,768]{2,3,1,0:T(8,128)(2,1)S(1)}, bf16[2,2,128,768]{2,3,1,0:T(8,128)(2,1)S(1)}, u32[]{:S(2)}, u32[]{:S(2)}) collective-permute-start(bf16[2,2,128,768]{2,3,1,0:T(8,128)(2,1)S(1)} %fusion.222), channel_id=1, source_target_pairs={{28,0},{0,4},{4,8},{8,12},{12,16},{16,20},{20,24},{24,28},{29,1},{... | collective-permute-start | bytes 2359304 | tf_op jit(solution)/shard_map/while/body/eval_jaxpr/ppermute | solution.py:20
  468.1 16.5 %copy-start.57 = (f32[12,32]{1,0:T(8,128)}, f32[12,32]{1,0:T(8,128)S(1)}, u32[]{:S(2)}) copy-start(f32[12,32]{1,0:T(8,128)S(1)} %fusion.224) | copy-start | bytes 4612 | tf_op jit(solution)/shard_map/while
  484.6 17.3 %collective-permute-start.1 = (bf16[2,2,128,768]{2,3,1,0:T(8,128)(2,1)}, bf16[2,2,128,768]{2,3,1,0:T(8,128)(2,1)S(1)}, u32[]{:S(2)}, u32[]{:S(2)}) collective-permute-start(bf16[2,2,128,768]{2,3,1,0:T(8,128)(2,1)} %get-tuple-element.1127), channel_id=1, source_target_pairs={{28,0},{0,4},{4,8},{8,12},{12,16},{16,20},{20,24},{24,28},{29,1},{... | collective-permute-start | bytes 2359304 | tf_op jit(solution)/shard_map/while/body/eval_jaxpr/ppermute | solution.py:20
  504.4 20.5 %collective-permute-start.2 = (bf16[2,2,128,768]{2,3,1,0:T(8,128)(2,1)S(1)}, bf16[2,2,128,768]{2,3,1,0:T(8,128)(2,1)S(1)}, u32[]{:S(2)}, u32[]{:S(2)}) collective-permute-start(bf16[2,2,128,768]{2,3,1,0:T(8,128)(2,1)S(1)} %fusion.222), channel_id=1, source_target_pairs={{28,0},{0,4},{4,8},{8,12},{12,16},{16,20},{20,24},{24,28},{29,1},{... | collective-permute-start | bytes 2359304 | tf_op jit(solution)/shard_map/while/body/eval_jaxpr/ppermute | solution.py:20
  506.2 18.6 %copy-start.57 = (f32[12,32]{1,0:T(8,128)}, f32[12,32]{1,0:T(8,128)S(1)}, u32[]{:S(2)}) copy-start(f32[12,32]{1,0:T(8,128)S(1)} %fusion.224) | copy-start | bytes 4612 | tf_op jit(solution)/shard_map/while
  524.9 19.4 %collective-permute-start.1 = (bf16[2,2,128,768]{2,3,1,0:T(8,128)(2,1)}, bf16[2,2,128,768]{2,3,1,0:T(8,128)(2,1)S(1)}, u32[]{:S(2)}, u32[]{:S(2)}) collective-permute-start(bf16[2,2,128,768]{2,3,1,0:T(8,128)(2,1)} %get-tuple-element.1127), channel_id=1, source_target_pairs={{28,0},{0,4},{4,8},{8,12},{12,16},{16,20},{20,24},{24,28},{29,1},{... | collective-permute-start | bytes 2359304 | tf_op jit(solution)/shard_map/while/body/eval_jaxpr/ppermute | solution.py:20
  546.8 22.8 %collective-permute-start.2 = (bf16[2,2,128,768]{2,3,1,0:T(8,128)(2,1)S(1)}, bf16[2,2,128,768]{2,3,1,0:T(8,128)(2,1)S(1)}, u32[]{:S(2)}, u32[]{:S(2)}) collective-permute-start(bf16[2,2,128,768]{2,3,1,0:T(8,128)(2,1)S(1)} %fusion.222), channel_id=1, source_target_pairs={{28,0},{0,4},{4,8},{8,12},{12,16},{16,20},{20,24},{24,28},{29,1},{... | collective-permute-start | bytes 2359304 | tf_op jit(solution)/shard_map/while/body/eval_jaxpr/ppermute | solution.py:20
  548.7 20.9 %copy-start.57 = (f32[12,32]{1,0:T(8,128)}, f32[12,32]{1,0:T(8,128)S(1)}, u32[]{:S(2)}) copy-start(f32[12,32]{1,0:T(8,128)S(1)} %fusion.224) | copy-start | bytes 4612 | tf_op jit(solution)/shard_map/while
  569.6 21.8 %collective-permute-start.1 = (bf16[2,2,128,768]{2,3,1,0:T(8,128)(2,1)}, bf16[2,2,128,768]{2,3,1,0:T(8,128)(2,1)S(1)}, u32[]{:S(2)}, u32[]{:S(2)}) collective-permute-start(bf16[2,2,128,768]{2,3,1,0:T(8,128)(2,1)} %get-tuple-element.1127), channel_id=1, source_target_pairs={{28,0},{0,4},{4,8},{8,12},{12,16},{16,20},{20,24},{24,28},{29,1},{... | collective-permute-start | bytes 2359304 | tf_op jit(solution)/shard_map/while/body/eval_jaxpr/ppermute | solution.py:20
  593.9 14.7 %collective-permute-start.2 = (bf16[2,2,128,768]{2,3,1,0:T(8,128)(2,1)S(1)}, bf16[2,2,128,768]{2,3,1,0:T(8,128)(2,1)S(1)}, u32[]{:S(2)}, u32[]{:S(2)}) collective-permute-start(bf16[2,2,128,768]{2,3,1,0:T(8,128)(2,1)S(1)} %fusion.222), channel_id=1, source_target_pairs={{28,0},{0,4},{4,8},{8,12},{12,16},{16,20},{20,24},{24,28},{29,1},{... | collective-permute-start | bytes 2359304 | tf_op jit(solution)/shard_map/while/body/eval_jaxpr/ppermute | solution.py:20
  595.7 12.9 %copy-start.57 = (f32[12,32]{1,0:T(8,128)}, f32[12,32]{1,0:T(8,128)S(1)}, u32[]{:S(2)}) copy-start(f32[12,32]{1,0:T(8,128)S(1)} %fusion.224) | copy-start | bytes 4612 | tf_op jit(solution)/shard_map/while
  611.2 53.4 %reduce-scatter.11.cloned.1.call-start = ((), (), s32[]{:S(2)}) async-start(), calls=%async_computation.14 | async-start | bytes 1474560 | tf_op jit(solution)/shard_map/reduce_scatter | solution.py:351
  612.9 80.7 %reduce-scatter.7.cloned.1.call-start = ((), (), s32[]{:S(2)}) async-start(), calls=%async_computation.12 | async-start | bytes 1474560 | tf_op jit(solution)/shard_map/reduce_scatter | solution.py:345
  615.0 129.0 %reduce-scatter.15.cloned.1.call-start = ((), (), s32[]{:S(2)}) async-start(), calls=%async_computation.16 | async-start | bytes 5898240 | tf_op jit(solution)/shard_map/reduce_scatter | solution.py:363
  620.3 174.1 %reduce-scatter.17.cloned.1.call-start = ((), (), s32[]{:S(2)}) async-start(), calls=%async_computation.17 | async-start | bytes 5898240 | tf_op jit(solution)/shard_map/reduce_scatter | solution.py:366
  630.5 12.0 %copy-start.55 = (f32[2,128]{1,0:T(2,128)S(1)}, f32[2,128]{1,0:T(2,128)}, u32[]{:S(2)}) copy-start(f32[2,128]{1,0:T(2,128)} %copy-done.54) | copy-start | bytes 3076
  630.5 12.0 %copy-start.3 = (f32[256,768]{1,0:T(8,128)S(1)}, f32[256,768]{1,0:T(8,128)}, u32[]{:S(2)}) copy-start(f32[256,768]{1,0:T(8,128)} %copy-done.2) | copy-start | bytes 2359300
  (89 other events, 147.6 us)
Sparse Core Ops, SparseCore 0:
  9.6 20.2 all-gather.10
  31.5 17.5 all-gather.6
  50.6 17.4 all-gather.8
  69.5 17.4 all-gather.12
  88.4 37.4 all-gather.14
  127.3 37.4 all-gather.16
  311.9 25.7 reduce-scatter.12
  611.4 24.8 reduce-scatter.8
  638.8 25.8 reduce-scatter.10
  667.8 25.7 reduce-scatter.6
  696.1 47.8 reduce-scatter.14
  746.5 47.7 reduce-scatter.16
where the time goes:
time: 1090 us; the launch traced here: 1080 us
  waiting for transfers between devices  554 us (51%)
  blocking collectives  341 us (31%)
  matrix products  97.1 us (9%)
  local copies, waits for them, and re-layouts  35.9 us (3%)
  other arithmetic  25.6 us (2%)
  between operations  20.7 us (2%)
    ppermute x22, waiting for transfers between devices, passed_along(): return lax.ppermute(block, axis, route)  371 us
    psum x1, blocking collectives, on_device(): lax.psum((shares[0], shares[1], shares[2], shares[3], shares[4], shares[5...  279 us
    reduce_scatter x1, waiting for transfers between devices, on_device(): lax.psum_scatter(local_grads[8].astype(jnp.bfloat16), 'wsh', scatter_dime...  50.4 us
    reduce_scatter x1, waiting for transfers between devices, on_device(): lax.psum_scatter(local_grads[7].astype(jnp.bfloat16), 'wsh', scatter_dime...  50.4 us
    psum x1, blocking collectives, on_device(): lax.psum((jnp.sum(deviation * deviation * row_valid), jnp.sum(row_valid))...  37.3 us
    reduce_scatter x1, waiting for transfers between devices, on_device(): lax.psum_scatter(local_grads[1].astype(jnp.bfloat16), 'wsh', scatter_dime...  28.9 us
  transfers between devices with their start and end apart: 34, of which 28 were waited for; matrix products, arithmetic and copies ran while one was open for 12% of the time, Pallas kernels for 0%

commit v1 on v0

--- a/solution.py
+++ b/solution.py
@@ -1,3 +1,4 @@
+import functools
 import jax
 import jax.numpy as jnp
 from jax import lax
@@ -12,6 +13,15 @@
 EPS = 1e-06
 NEG_FILL = -1e30
 BUCKET_EDGES = (12, 16, 23, 32, 46, 64, 91)
+
+
+def run_squares(message, dev_axis, axis_id):
+    for at in (dev_axis, axis_id):
+        message = lax.psum(message, at)
+    return message
+
+
+state_pieces_all = functools.partial(run_squares, dev_axis="ctx", axis_id="wsh")
 
 
 def passed_along(block, axis, distance):
@@ -221,8 +231,8 @@
         (query_places[None, :] < seq_lengths[:, None]).astype(jnp.float32).reshape(row_count, 1)
     )
     deviation = result - teacher.reshape(row_count, D).astype(jnp.float32)
-    square_sum, valid_count = lax.psum(
-        (jnp.sum(deviation * deviation * row_valid), jnp.sum(row_valid)), ("ctx", "wsh")
+    square_sum, valid_count = state_pieces_all(
+        (jnp.sum(deviation * deviation * row_valid), jnp.sum(row_valid))
     )
     loss_value = square_sum / (valid_count * D)
     result_grad = token_total / valid_count * deviation * row_valid

time: 1090 us -> 1060 us (0.972)
  waiting for transfers between devices: 554 us -> 533 us
    all_gather x1, waiting for transfers between devices: 14 us -> 0.01 us  [on_device(): lax.all_gather(shards[3], 'wsh', axis=0, tiled=True)]
    all_gather x1, waiting for transfers between devices: 14 us -> 0.02 us  [on_device(): lax.all_gather(shards[2], 'wsh', axis=0, tiled=True)]
    psum x2 -> x4, blocking collectives: 316 us -> 315 us  [run_squares(): message = lax.psum(message, at)]
  transfers between devices with their start and end apart: 34 -> 34, of which waited for: 28 -> 26; matrix products, arithmetic and copies ran while one was open for 12% -> 12% of each run, Pallas kernels for 0% -> 0%
where the time goes in v1:
time: 1060 us; the launch traced here: 1050 us
  waiting for transfers between devices  533 us (50%)
  blocking collectives  339 us (32%)
  matrix products  96.1 us (9%)
  local copies, waits for them, and re-layouts  35.7 us (3%)
  other arithmetic  24.3 us (2%)
  between operations  20.7 us (2%)
    ppermute x22, waiting for transfers between devices, passed_along(): return lax.ppermute(block, axis, route)  377 us
    psum x4, blocking collectives, run_squares(): message = lax.psum(message, at)  315 us
    reduce_scatter x1, waiting for transfers between devices, on_device(): lax.psum_scatter(local_grads[7].astype(jnp.bfloat16), 'wsh', scatter_dime...  50.4 us
    reduce_scatter x1, waiting for transfers between devices, on_device(): lax.psum_scatter(local_grads[8].astype(jnp.bfloat16), 'wsh', scatter_dime...  50.4 us
    reduce_scatter x1, waiting for transfers between devices, on_device(): lax.psum_scatter(local_grads[1].astype(jnp.bfloat16), 'wsh', scatter_dime...  28.9 us
    reduce_scatter x1, waiting for transfers between devices, on_device(): lax.psum_scatter(local_grads[3].astype(jnp.bfloat16), 'wsh', scatter_dime...  22.5 us
  transfers between devices with their start and end apart: 34, of which 26 were waited for; matrix products, arithmetic and copies ran while one was open for 12% of the time, Pallas kernels for 0%

profile of v1, /device:TPU:0, one launch (start us, length us, event | category | flops | bytes accessed | tf_op | source)
XLA Modules:
  0.0 1051.9 jit_solution(11832547324350513851)
XLA Ops:
  13.8 8.3 all-reduce.7
  22.3 5.2 all_gather.31
  28.3 1.1 copy.159
  30.8 22.3 %psum.93 = f32[]{:T(128)} all-reduce(f32[]{:T(128)} %get-tuple-element.854), channel_id=1, replica_groups=mesh['ctx'=8,'wsh'=4] {'ctx'}, use_global_device_ids=true, to_apply=%region_12.13 | all-reduce | flops 1 | bytes 8 | tf_op jit(solution)/shard_map/psum | solution.py:20
  53.6 7.0 psum.94
  63.0 1.8 convolution_convert_fusion.9
  65.1 1.9 convolution_convert_fusion.11
  67.3 1.7 fusion.112
  70.2 1.7 convolution_convert_fusion.10
  74.1 151.0 %while.44 = (s32[]{:T(128)}, bf16[2,2,128,768]{2,3,1,0:T(8,128)(2,1)}, f32[2,12,128]{2,1,0:T(8,128)S(1)}, f32[2,12,128]{2,1,0:T(8,128)}, f32[2,128,12,64]{1,3,2,...) while((s32[]{:T(128)}, ...), condition=%wide.region_6.7_spmd.clone, body=%wide.region_3.6_spmd.clone.sunk | while | flops 117384720 | bytes 21013696 | solution.py:211
  76.1 20.1 %collective-permute-done = bf16[2,2,128,768]{2,3,1,0:T(8,128)(2,1)S(1)} collective-permute-done((bf16[2,2,128,768]{2,3,1,0:T(8,128)(2,1)}, bf16[2,2,128,768]{2,3,1,0:T(8,128)(2,1)S(1)}, u32[]{:S(2)}, u32[]{:S(2)}) %collective-permute-start) | collective-permute-done | bytes 786464 | tf_op jit(solution)/shard_map/while/body/eval_jaxpr/ppermute | solution.py:30
  100.4 19.2 %collective-permute-done = bf16[2,2,128,768]{2,3,1,0:T(8,128)(2,1)S(1)} collective-permute-done((bf16[2,2,128,768]{2,3,1,0:T(8,128)(2,1)}, bf16[2,2,128,768]{2,3,1,0:T(8,128)(2,1)S(1)}, u32[]{:S(2)}, u32[]{:S(2)}) %collective-permute-start) | collective-permute-done | bytes 786464 | tf_op jit(solution)/shard_map/while/body/eval_jaxpr/ppermute | solution.py:30
  123.8 18.3 %collective-permute-done = bf16[2,2,128,768]{2,3,1,0:T(8,128)(2,1)S(1)} collective-permute-done((bf16[2,2,128,768]{2,3,1,0:T(8,128)(2,1)}, bf16[2,2,128,768]{2,3,1,0:T(8,128)(2,1)S(1)}, u32[]{:S(2)}, u32[]{:S(2)}) %collective-permute-start) | collective-permute-done | bytes 786464 | tf_op jit(solution)/shard_map/while/body/eval_jaxpr/ppermute | solution.py:30
  146.3 17.4 %collective-permute-done = bf16[2,2,128,768]{2,3,1,0:T(8,128)(2,1)S(1)} collective-permute-done((bf16[2,2,128,768]{2,3,1,0:T(8,128)(2,1)}, bf16[2,2,128,768]{2,3,1,0:T(8,128)(2,1)S(1)}, u32[]{:S(2)}, u32[]{:S(2)}) %collective-permute-start) | collective-permute-done | bytes 786464 | tf_op jit(solution)/shard_map/while/body/eval_jaxpr/ppermute | solution.py:30
  167.9 16.5 %collective-permute-done = bf16[2,2,128,768]{2,3,1,0:T(8,128)(2,1)S(1)} collective-permute-done((bf16[2,2,128,768]{2,3,1,0:T(8,128)(2,1)}, bf16[2,2,128,768]{2,3,1,0:T(8,128)(2,1)S(1)}, u32[]{:S(2)}, u32[]{:S(2)}) %collective-permute-start) | collective-permute-done | bytes 786464 | tf_op jit(solution)/shard_map/while/body/eval_jaxpr/ppermute | solution.py:30
  188.5 15.5 %collective-permute-done = bf16[2,2,128,768]{2,3,1,0:T(8,128)(2,1)S(1)} collective-permute-done((bf16[2,2,128,768]{2,3,1,0:T(8,128)(2,1)}, bf16[2,2,128,768]{2,3,1,0:T(8,128)(2,1)S(1)}, u32[]{:S(2)}, u32[]{:S(2)}) %collective-permute-start) | collective-permute-done | bytes 786464 | tf_op jit(solution)/shard_map/while/body/eval_jaxpr/ppermute | solution.py:30
  208.3 14.6 %collective-permute-done = bf16[2,2,128,768]{2,3,1,0:T(8,128)(2,1)S(1)} collective-permute-done((bf16[2,2,128,768]{2,3,1,0:T(8,128)(2,1)}, bf16[2,2,128,768]{2,3,1,0:T(8,128)(2,1)S(1)}, u32[]{:S(2)}, u32[]{:S(2)}) %collective-permute-start) | collective-permute-done | bytes 786464 | tf_op jit(solution)/shard_map/while/body/eval_jaxpr/ppermute | solution.py:30
  225.9 1.7 fusion.106
  227.6 2.1 multiply_reduce_fusion.4
  230.4 11.3 %multiply_convert_fusion.1 = (bf16[256,3072]{1,0:T(8,128)(2,1)S(1)}, f32[256,3072]{1,0:T(8,128)}, f32[256,3072]{1,0:T(8,128)}) fusion(bf16[768,3072]{1,0:T(8,128)(2,1)} %all-gather.15.cloned.1.call-done, f32[256,768]{1,0:T(8,128)S(1)} %get-tuple-element.884, f32[768]{0:T(1024)S(1)} %copy-done.42, f32[256]{0:T(256)S(1)} %fusion.98), kind=kOutput, calls=%fused_computation.67 | convolution fusion | flops 1259667456 | bytes 13373440 | tf_op jit(solution)/shard_map/dot_general | solution.py:226
  241.8 4.3 fusion.71
  246.2 5.2 add_convert_fusion
  251.5 2.1 multiply_reduce_fusion
  253.6 2.6 fusion.57
  258.8 1.6 multiply_reduce_fusion.1
  261.2 1.4 convert_reduce_fusion.1
  264.6 1.1 copy.198
  265.8 2.6 convolution_convert_fusion.2
  268.4 2.1 fusion.49
  270.9 10.9 %collective-permute-done.3 = bf16[2,2,128,768]{2,3,1,0:T(8,128)(2,1)S(1)} collective-permute-done((bf16[2,2,128,768]{2,3,1,0:T(8,128)(2,1)}, bf16[2,2,128,768]{2,3,1,0:T(8,128)(2,1)S(1)}, u32[]{:S(2)}, u32[]{:S(2)}) %collective-permute-start.3) | collective-permute-done | bytes 786464 | tf_op jit(solution)/shard_map/ppermute | solution.py:30
  281.8 291.3 %while.45 = (s32[]{:T(128)}, bf16[2,2,128,768]{2,3,1,0:T(8,128)(2,1)}, bf16[2,2,128,768]{2,3,1,0:T(8,128)(2,1)S(1)}, f32[2,128,12,64]{1,3,2,0:T(8,128)S(1)}, f32...) while((s32[]{:T(128)}, ...), condition=%wide.region_19.20_spmd.clone, body=%wide.region_17.19_spmd.clone.sunk | while | flops 283444096 | bytes 33844516 | solution.py:318
  282.2 1.1 fusion.219
  283.7 14.1 %collective-permute-done.1 = bf16[2,2,128,768]{2,3,1,0:T(8,128)(2,1)S(1)} collective-permute-done((bf16[2,2,128,768]{2,3,1,0:T(8,128)(2,1)}, bf16[2,2,128,768]{2,3,1,0:T(8,128)(2,1)S(1)}, u32[]{:S(2)}, u32[]{:S(2)}) %collective-permute-start.1) | collective-permute-done | bytes 786464 | tf_op jit(solution)/shard_map/while/body/eval_jaxpr/ppermute | solution.py:30
  302.8 16.5 %collective-permute-done.2 = bf16[2,2,128,768]{2,3,1,0:T(8,128)(2,1)S(1)} collective-permute-done((bf16[2,2,128,768]{2,3,1,0:T(8,128)(2,1)S(1)}, bf16[2,2,128,768]{2,3,1,0:T(8,128)(2,1)S(1)}, u32[]{:S(2)}, u32[]{:S(2)}) %collective-permute-start.2) | collective-permute-done | bytes 786464 | tf_op jit(solution)/shard_map/while/body/eval_jaxpr/ppermute | solution.py:30
  319.4 1.1 fusion.219
  320.9 16.3 %collective-permute-done.1 = bf16[2,2,128,768]{2,3,1,0:T(8,128)(2,1)S(1)} collective-permute-done((bf16[2,2,128,768]{2,3,1,0:T(8,128)(2,1)}, bf16[2,2,128,768]{2,3,1,0:T(8,128)(2,1)S(1)}, u32[]{:S(2)}, u32[]{:S(2)}) %collective-permute-start.1) | collective-permute-done | bytes 786464 | tf_op jit(solution)/shard_map/while/body/eval_jaxpr/ppermute | solution.py:30
  342.2 18.6 %collective-permute-done.2 = bf16[2,2,128,768]{2,3,1,0:T(8,128)(2,1)S(1)} collective-permute-done((bf16[2,2,128,768]{2,3,1,0:T(8,128)(2,1)S(1)}, bf16[2,2,128,768]{2,3,1,0:T(8,128)(2,1)S(1)}, u32[]{:S(2)}, u32[]{:S(2)}) %collective-permute-start.2) | collective-permute-done | bytes 786464 | tf_op jit(solution)/shard_map/while/body/eval_jaxpr/ppermute | solution.py:30
  360.9 1.1 fusion.219
  362.4 18.4 %collective-permute-done.1 = bf16[2,2,128,768]{2,3,1,0:T(8,128)(2,1)S(1)} collective-permute-done((bf16[2,2,128,768]{2,3,1,0:T(8,128)(2,1)}, bf16[2,2,128,768]{2,3,1,0:T(8,128)(2,1)S(1)}, u32[]{:S(2)}, u32[]{:S(2)}) %collective-permute-start.1) | collective-permute-done | bytes 786464 | tf_op jit(solution)/shard_map/while/body/eval_jaxpr/ppermute | solution.py:30
  385.8 20.4 %collective-permute-done.2 = bf16[2,2,128,768]{2,3,1,0:T(8,128)(2,1)S(1)} collective-permute-done((bf16[2,2,128,768]{2,3,1,0:T(8,128)(2,1)S(1)}, bf16[2,2,128,768]{2,3,1,0:T(8,128)(2,1)S(1)}, u32[]{:S(2)}, u32[]{:S(2)}) %collective-permute-start.2) | collective-permute-done | bytes 786464 | tf_op jit(solution)/shard_map/while/body/eval_jaxpr/ppermute | solution.py:30
  406.4 1.1 fusion.219
  407.9 20.4 %collective-permute-done.1 = bf16[2,2,128,768]{2,3,1,0:T(8,128)(2,1)S(1)} collective-permute-done((bf16[2,2,128,768]{2,3,1,0:T(8,128)(2,1)}, bf16[2,2,128,768]{2,3,1,0:T(8,128)(2,1)S(1)}, u32[]{:S(2)}, u32[]{:S(2)}) %collective-permute-start.1) | collective-permute-done | bytes 786464 | tf_op jit(solution)/shard_map/while/body/eval_jaxpr/ppermute | solution.py:30
  433.3 18.5 %collective-permute-done.2 = bf16[2,2,128,768]{2,3,1,0:T(8,128)(2,1)S(1)} collective-permute-done((bf16[2,2,128,768]{2,3,1,0:T(8,128)(2,1)S(1)}, bf16[2,2,128,768]{2,3,1,0:T(8,128)(2,1)S(1)}, u32[]{:S(2)}, u32[]{:S(2)}) %collective-permute-start.2) | collective-permute-done | bytes 786464 | tf_op jit(solution)/shard_map/while/body/eval_jaxpr/ppermute | solution.py:30
  452.0 1.1 fusion.219
  453.4 20.9 %collective-permute-done.1 = bf16[2,2,128,768]{2,3,1,0:T(8,128)(2,1)S(1)} collective-permute-done((bf16[2,2,128,768]{2,3,1,0:T(8,128)(2,1)}, bf16[2,2,128,768]{2,3,1,0:T(8,128)(2,1)S(1)}, u32[]{:S(2)}, u32[]{:S(2)}) %collective-permute-start.1) | collective-permute-done | bytes 786464 | tf_op jit(solution)/shard_map/while/body/eval_jaxpr/ppermute | solution.py:30
  479.4 16.8 %collective-permute-done.2 = bf16[2,2,128,768]{2,3,1,0:T(8,128)(2,1)S(1)} collective-permute-done((bf16[2,2,128,768]{2,3,1,0:T(8,128)(2,1)S(1)}, bf16[2,2,128,768]{2,3,1,0:T(8,128)(2,1)S(1)}, u32[]{:S(2)}, u32[]{:S(2)}) %collective-permute-start.2) | collective-permute-done | bytes 786464 | tf_op jit(solution)/shard_map/while/body/eval_jaxpr/ppermute | solution.py:30
  496.3 1.1 fusion.219
  497.8 19.2 %collective-permute-done.1 = bf16[2,2,128,768]{2,3,1,0:T(8,128)(2,1)S(1)} collective-permute-done((bf16[2,2,128,768]{2,3,1,0:T(8,128)(2,1)}, bf16[2,2,128,768]{2,3,1,0:T(8,128)(2,1)S(1)}, u32[]{:S(2)}, u32[]{:S(2)}) %collective-permute-start.1) | collective-permute-done | bytes 786464 | tf_op jit(solution)/shard_map/while/body/eval_jaxpr/ppermute | solution.py:30
  521.9 14.9 %collective-permute-done.2 = bf16[2,2,128,768]{2,3,1,0:T(8,128)(2,1)S(1)} collective-permute-done((bf16[2,2,128,768]{2,3,1,0:T(8,128)(2,1)S(1)}, bf16[2,2,128,768]{2,3,1,0:T(8,128)(2,1)S(1)}, u32[]{:S(2)}, u32[]{:S(2)}) %collective-permute-start.2) | collective-permute-done | bytes 786464 | tf_op jit(solution)/shard_map/while/body/eval_jaxpr/ppermute | solution.py:30
  538.5 17.3 %collective-permute-done.1 = bf16[2,2,128,768]{2,3,1,0:T(8,128)(2,1)S(1)} collective-permute-done((bf16[2,2,128,768]{2,3,1,0:T(8,128)(2,1)}, bf16[2,2,128,768]{2,3,1,0:T(8,128)(2,1)S(1)}, u32[]{:S(2)}, u32[]{:S(2)}) %collective-permute-start.1) | collective-permute-done | bytes 786464 | tf_op jit(solution)/shard_map/while/body/eval_jaxpr/ppermute | solution.py:30
  560.8 12.2 %collective-permute-done.2 = bf16[2,2,128,768]{2,3,1,0:T(8,128)(2,1)S(1)} collective-permute-done((bf16[2,2,128,768]{2,3,1,0:T(8,128)(2,1)S(1)}, bf16[2,2,128,768]{2,3,1,0:T(8,128)(2,1)S(1)}, u32[]{:S(2)}, u32[]{:S(2)}) %collective-permute-start.2) | collective-permute-done | bytes 786464 | tf_op jit(solution)/shard_map/while/body/eval_jaxpr/ppermute | solution.py:30
  574.1 1.6 convolution_convert_fusion.4
  575.7 1.5 convolution_convert_fusion.3
  577.9 1.5 convolution_convert_fusion.5
  579.5 3.6 convolution_convert_fusion
  584.8 3.7 convolution_convert_fusion.1
  591.4 1.5 convolution_add_fusion.1
  593.6 10.3 all-reduce.6
  605.2 22.5 %reduce-scatter.11.cloned.1.call-done = bf16[192,768]{1,0:T(8,128)(2,1)} async-done(((bf16[768,768]{1,0:T(8,128)(2,1)}), bf16[192,768]{1,0:T(8,128)(2,1)}) %reduce-scatter.11.cloned.1.call-update) | async-done | bytes 294928 | tf_op jit(solution)/shard_map/reduce_scatter | solution.py:361
  627.7 28.9 %reduce-scatter.7.cloned.1.call-done = bf16[192,768]{1,0:T(8,128)(2,1)} async-done(((bf16[768,768]{1,0:T(8,128)(2,1)}), bf16[192,768]{1,0:T(8,128)(2,1)}) %reduce-scatter.7.cloned.1.call-update) | async-done | bytes 294928 | tf_op jit(solution)/shard_map/reduce_scatter | solution.py:355
  656.6 50.4 %reduce-scatter.17.cloned.1.call-done = bf16[768,768]{1,0:T(8,128)(2,1)} async-done(((bf16[3072,768]{1,0:T(8,128)(2,1)}), bf16[768,768]{1,0:T(8,128)(2,1)}) %reduce-scatter.17.cloned.1.call-update) | async-done | bytes 1179664 | tf_op jit(solution)/shard_map/reduce_scatter | solution.py:376
  707.0 50.4 %reduce-scatter.15.cloned.1.call-done = bf16[192,3072]{1,0:T(8,128)(2,1)} async-done(((bf16[768,3072]{1,0:T(8,128)(2,1)}), bf16[192,3072]{1,0:T(8,128)(2,1)}) %reduce-scatter.15.cloned.1.call-update) | async-done | bytes 1179664 | tf_op jit(solution)/shard_map/reduce_scatter | solution.py:373
  757.4 279.0 %all-reduce.9 = (f32[]{:T(128)}, f32[192]{0:T(256)}, f32[192,768]{1,0:T(8,128)}, f32[192,768]{1,0:T(8,128)}, f32[192,768]{1,0:T(8,128)}, /*index=5*/f32[192,768]...) all-reduce(f32[]{:T(128)} %get-tuple-element.873, ...), channel_id=1, replica_groups=mesh['ctx'=8,'wsh'=4] {'ctx'}, use_global_device_ids=true, to_apply=%region_9.10 | all-reduce | flops 1769953 | bytes 10620680 | tf_op jit(solution)/shard_map/psum | solution.py:20
  1036.5 6.5 psum.92
  (569 shorter events, 94.4 us)
Async XLA Ops:
  7.2 4.8 copy-start.59
  7.2 4.1 copy-start.4
  7.2 6.1 copy-start.65
  7.2 6.3 copy-start.66
  7.2 15.1 %copy-start.58 = (bf16[8,12]{1,0:T(8,128)(2,1)S(1)}, bf16[8,12]{1,0:T(8,128)(2,1)}, u32[]{:S(2)}) copy-start(bf16[8,12]{1,0:T(8,128)(2,1)} %param.24) | copy-start | bytes 580
  7.2 55.8 %all-gather.11.cloned.1.call-start = ((), (), s32[]{:S(2)}) async-start(), calls=%async_computation.8 | async-start | bytes 1474560 | tf_op jit(solution)/shard_map/all_gather | solution.py:97
  8.0 57.1 %all-gather.7.cloned.1.call-start = ((), (), s32[]{:S(2)}) async-start(), calls=%async_computation.6 | async-start | bytes 1474560 | tf_op jit(solution)/shard_map/all_gather | solution.py:98
  8.7 61.5 %all-gather.9.cloned.1.call-start = ((), (), s32[]{:S(2)}) async-start(), calls=%async_computation.7 | async-start | bytes 1474560 | tf_op jit(solution)/shard_map/all_gather | solution.py:99
  9.5 218.1 %all-gather.13.cloned.1.call-start = ((), (), s32[]{:S(2)}) async-start(), calls=%async_computation.9 | async-start | bytes 1474560 | tf_op jit(solution)/shard_map/all_gather | solution.py:100
  10.0 220.4 %all-gather.15.cloned.1.call-start = ((), (), s32[]{:S(2)}) async-start(), calls=%async_computation.10 | async-start | bytes 5898240 | tf_op jit(solution)/shard_map/all_gather | solution.py:103
  10.6 231.1 %all-gather.17.cloned.1.call-start = ((), (), s32[]{:S(2)}) async-start(), calls=%async_computation.11 | async-start | bytes 5898240 | tf_op jit(solution)/shard_map/all_gather | solution.py:104
  11.2 594.0 %reduce-scatter.13.cloned.1.call-start = ((), (), s32[]{:S(2)}) async-start(), calls=%async_computation.15 | async-start | bytes 1474560 | tf_op jit(solution)/shard_map/reduce_scatter | solution.py:364
  12.0 49.2 %copy-start.49 = (f32[256]{0:T(256)}, f32[256]{0:T(256)S(1)}, u32[]{:S(2)}) copy-start(f32[256]{0:T(256)S(1)} %bitcast_rsqrt_fusion) | copy-start | bytes 3076
  22.1 39.2 %copy-start.45 = (f32[768]{0:T(1024)}, f32[768]{0:T(1024)S(1)}, u32[]{:S(2)}) copy-start(f32[768]{0:T(1024)S(1)} %convert_element_type.491) | copy-start | bytes 9220
  22.3 5.7 copy-start.41
  69.1 4.6 copy-start
  74.1 22.1 %collective-permute-start = (bf16[2,2,128,768]{2,3,1,0:T(8,128)(2,1)}, bf16[2,2,128,768]{2,3,1,0:T(8,128)(2,1)S(1)}, u32[]{:S(2)}, u32[]{:S(2)}) collective-permute-start(bf16[2,2,128,768]{2,3,1,0:T(8,128)(2,1)} %get-tuple-element.1078), channel_id=1, source_target_pairs={{28,0},{0,4},{4,8},{8,12},{12,16},{16,20},{20,24},{24,28},{29,1},{... | collective-permute-start | bytes 2359304 | tf_op jit(solution)/shard_map/while/body/eval_jaxpr/ppermute | solution.py:30
  98.5 21.2 %collective-permute-start = (bf16[2,2,128,768]{2,3,1,0:T(8,128)(2,1)}, bf16[2,2,128,768]{2,3,1,0:T(8,128)(2,1)S(1)}, u32[]{:S(2)}, u32[]{:S(2)}) collective-permute-start(bf16[2,2,128,768]{2,3,1,0:T(8,128)(2,1)} %get-tuple-element.1078), channel_id=1, source_target_pairs={{28,0},{0,4},{4,8},{8,12},{12,16},{16,20},{20,24},{24,28},{29,1},{... | collective-permute-start | bytes 2359304 | tf_op jit(solution)/shard_map/while/body/eval_jaxpr/ppermute | solution.py:30
  121.9 20.2 %collective-permute-start = (bf16[2,2,128,768]{2,3,1,0:T(8,128)(2,1)}, bf16[2,2,128,768]{2,3,1,0:T(8,128)(2,1)S(1)}, u32[]{:S(2)}, u32[]{:S(2)}) collective-permute-start(bf16[2,2,128,768]{2,3,1,0:T(8,128)(2,1)} %get-tuple-element.1078), channel_id=1, source_target_pairs={{28,0},{0,4},{4,8},{8,12},{12,16},{16,20},{20,24},{24,28},{29,1},{... | collective-permute-start | bytes 2359304 | tf_op jit(solution)/shard_map/while/body/eval_jaxpr/ppermute | solution.py:30
  144.4 19.3 %collective-permute-start = (bf16[2,2,128,768]{2,3,1,0:T(8,128)(2,1)}, bf16[2,2,128,768]{2,3,1,0:T(8,128)(2,1)S(1)}, u32[]{:S(2)}, u32[]{:S(2)}) collective-permute-start(bf16[2,2,128,768]{2,3,1,0:T(8,128)(2,1)} %get-tuple-element.1078), channel_id=1, source_target_pairs={{28,0},{0,4},{4,8},{8,12},{12,16},{16,20},{20,24},{24,28},{29,1},{... | collective-permute-start | bytes 2359304 | tf_op jit(solution)/shard_map/while/body/eval_jaxpr/ppermute | solution.py:30
  166.0 18.4 %collective-permute-start = (bf16[2,2,128,768]{2,3,1,0:T(8,128)(2,1)}, bf16[2,2,128,768]{2,3,1,0:T(8,128)(2,1)S(1)}, u32[]{:S(2)}, u32[]{:S(2)}) collective-permute-start(bf16[2,2,128,768]{2,3,1,0:T(8,128)(2,1)} %get-tuple-element.1078), channel_id=1, source_target_pairs={{28,0},{0,4},{4,8},{8,12},{12,16},{16,20},{20,24},{24,28},{29,1},{... | collective-permute-start | bytes 2359304 | tf_op jit(solution)/shard_map/while/body/eval_jaxpr/ppermute | solution.py:30
  186.6 17.5 %collective-permute-start = (bf16[2,2,128,768]{2,3,1,0:T(8,128)(2,1)}, bf16[2,2,128,768]{2,3,1,0:T(8,128)(2,1)S(1)}, u32[]{:S(2)}, u32[]{:S(2)}) collective-permute-start(bf16[2,2,128,768]{2,3,1,0:T(8,128)(2,1)} %get-tuple-element.1078), channel_id=1, source_target_pairs={{28,0},{0,4},{4,8},{8,12},{12,16},{16,20},{20,24},{24,28},{29,1},{... | collective-permute-start | bytes 2359304 | tf_op jit(solution)/shard_map/while/body/eval_jaxpr/ppermute | solution.py:30
  206.3 16.5 %collective-permute-start = (bf16[2,2,128,768]{2,3,1,0:T(8,128)(2,1)}, bf16[2,2,128,768]{2,3,1,0:T(8,128)(2,1)S(1)}, u32[]{:S(2)}, u32[]{:S(2)}) collective-permute-start(bf16[2,2,128,768]{2,3,1,0:T(8,128)(2,1)} %get-tuple-element.1078), channel_id=1, source_target_pairs={{28,0},{0,4},{4,8},{8,12},{12,16},{16,20},{20,24},{24,28},{29,1},{... | collective-permute-start | bytes 2359304 | tf_op jit(solution)/shard_map/while/body/eval_jaxpr/ppermute | solution.py:30
  229.7 23.9 %copy-start.14 = (f32[256,768]{1,0:T(8,128)}, f32[256,768]{1,0:T(8,128)S(1)}, u32[]{:S(2)}) copy-start(f32[256,768]{1,0:T(8,128)S(1)} %get-tuple-element.884) | copy-start | bytes 2359300
  229.7 21.7 %copy-start.53 = (f32[256]{0:T(256)}, f32[256]{0:T(256)S(1)}, u32[]{:S(2)}) copy-start(f32[256]{0:T(256)S(1)} %fusion.98) | copy-start | bytes 3076
  230.4 11.4 %copy-start.39 = (bf16[2,128,768]{2,1,0:T(8,128)(2,1)S(1)}, bf16[2,128,768]{2,1,0:T(8,128)(2,1)}, u32[]{:S(2)}) copy-start(bf16[2,128,768]{2,1,0:T(8,128)(2,1)} %param.17) | copy-start | bytes 1179652
  230.4 11.4 %copy-start.61 = (f32[256]{0:T(256)S(1)}, f32[256]{0:T(256)}, u32[]{:S(2)}) copy-start(f32[256]{0:T(256)} %convert_bitcast_fusion.1) | copy-start | bytes 3076
  241.7 4.4 copy-start.19
  241.8 4.4 copy-start.64
  241.8 9.6 slice-start
  246.1 5.3 copy-start.37
  246.1 5.3 slice-start.1
  256.2 9.6 copy-start.2
  264.3 17.5 %collective-permute-start.3 = (bf16[2,2,128,768]{2,3,1,0:T(8,128)(2,1)}, bf16[2,2,128,768]{2,3,1,0:T(8,128)(2,1)S(1)}, u32[]{:S(2)}, u32[]{:S(2)}) collective-permute-start(bf16[2,2,128,768]{2,3,1,0:T(8,128)(2,1)} %pad_maximum_fusion.1), channel_id=1, source_target_pairs={{28,0},{0,4},{4,8},{8,12},{12,16},{16,20},{20,24},{24,28},{29,1},{... | collective-permute-start | bytes 2359304 | tf_op jit(solution)/shard_map/ppermute | solution.py:30
  265.8 4.8 copy-start.7
  265.8 4.8 copy-start.22
  268.4 336.8 %reduce-scatter.9.cloned.1.call-start = ((), (), s32[]{:S(2)}) async-start(), calls=%async_computation.13 | async-start | bytes 1474560 | tf_op jit(solution)/shard_map/reduce_scatter | solution.py:358
  282.0 15.8 %collective-permute-start.1 = (bf16[2,2,128,768]{2,3,1,0:T(8,128)(2,1)}, bf16[2,2,128,768]{2,3,1,0:T(8,128)(2,1)S(1)}, u32[]{:S(2)}, u32[]{:S(2)}) collective-permute-start(bf16[2,2,128,768]{2,3,1,0:T(8,128)(2,1)} %get-tuple-element.1127), channel_id=1, source_target_pairs={{28,0},{0,4},{4,8},{8,12},{12,16},{16,20},{20,24},{24,28},{29,1},{... | collective-permute-start | bytes 2359304 | tf_op jit(solution)/shard_map/while/body/eval_jaxpr/ppermute | solution.py:30
  300.3 19.0 %collective-permute-start.2 = (bf16[2,2,128,768]{2,3,1,0:T(8,128)(2,1)S(1)}, bf16[2,2,128,768]{2,3,1,0:T(8,128)(2,1)S(1)}, u32[]{:S(2)}, u32[]{:S(2)}) collective-permute-start(bf16[2,2,128,768]{2,3,1,0:T(8,128)(2,1)S(1)} %fusion.222), channel_id=1, source_target_pairs={{28,0},{0,4},{4,8},{8,12},{12,16},{16,20},{20,24},{24,28},{29,1},{... | collective-permute-start | bytes 2359304 | tf_op jit(solution)/shard_map/while/body/eval_jaxpr/ppermute | solution.py:30
  302.1 17.1 %copy-start.56 = (f32[12,32]{1,0:T(8,128)}, f32[12,32]{1,0:T(8,128)S(1)}, u32[]{:S(2)}) copy-start(f32[12,32]{1,0:T(8,128)S(1)} %fusion.224) | copy-start | bytes 4612 | tf_op jit(solution)/shard_map/while
  319.2 17.9 %collective-permute-start.1 = (bf16[2,2,128,768]{2,3,1,0:T(8,128)(2,1)}, bf16[2,2,128,768]{2,3,1,0:T(8,128)(2,1)S(1)}, u32[]{:S(2)}, u32[]{:S(2)}) collective-permute-start(bf16[2,2,128,768]{2,3,1,0:T(8,128)(2,1)} %get-tuple-element.1127), channel_id=1, source_target_pairs={{28,0},{0,4},{4,8},{8,12},{12,16},{16,20},{20,24},{24,28},{29,1},{... | collective-permute-start | bytes 2359304 | tf_op jit(solution)/shard_map/while/body/eval_jaxpr/ppermute | solution.py:30
  339.6 21.1 %collective-permute-start.2 = (bf16[2,2,128,768]{2,3,1,0:T(8,128)(2,1)S(1)}, bf16[2,2,128,768]{2,3,1,0:T(8,128)(2,1)S(1)}, u32[]{:S(2)}, u32[]{:S(2)}) collective-permute-start(bf16[2,2,128,768]{2,3,1,0:T(8,128)(2,1)S(1)} %fusion.222), channel_id=1, source_target_pairs={{28,0},{0,4},{4,8},{8,12},{12,16},{16,20},{20,24},{24,28},{29,1},{... | collective-permute-start | bytes 2359304 | tf_op jit(solution)/shard_map/while/body/eval_jaxpr/ppermute | solution.py:30
  341.5 19.3 %copy-start.56 = (f32[12,32]{1,0:T(8,128)}, f32[12,32]{1,0:T(8,128)S(1)}, u32[]{:S(2)}) copy-start(f32[12,32]{1,0:T(8,128)S(1)} %fusion.224) | copy-start | bytes 4612 | tf_op jit(solution)/shard_map/while
  360.8 20.1 %collective-permute-start.1 = (bf16[2,2,128,768]{2,3,1,0:T(8,128)(2,1)}, bf16[2,2,128,768]{2,3,1,0:T(8,128)(2,1)S(1)}, u32[]{:S(2)}, u32[]{:S(2)}) collective-permute-start(bf16[2,2,128,768]{2,3,1,0:T(8,128)(2,1)} %get-tuple-element.1127), channel_id=1, source_target_pairs={{28,0},{0,4},{4,8},{8,12},{12,16},{16,20},{20,24},{24,28},{29,1},{... | collective-permute-start | bytes 2359304 | tf_op jit(solution)/shard_map/while/body/eval_jaxpr/ppermute | solution.py:30
  383.3 23.0 %collective-permute-start.2 = (bf16[2,2,128,768]{2,3,1,0:T(8,128)(2,1)S(1)}, bf16[2,2,128,768]{2,3,1,0:T(8,128)(2,1)S(1)}, u32[]{:S(2)}, u32[]{:S(2)}) collective-permute-start(bf16[2,2,128,768]{2,3,1,0:T(8,128)(2,1)S(1)} %fusion.222), channel_id=1, source_target_pairs={{28,0},{0,4},{4,8},{8,12},{12,16},{16,20},{20,24},{24,28},{29,1},{... | collective-permute-start | bytes 2359304 | tf_op jit(solution)/shard_map/while/body/eval_jaxpr/ppermute | solution.py:30
  385.2 21.1 %copy-start.56 = (f32[12,32]{1,0:T(8,128)}, f32[12,32]{1,0:T(8,128)S(1)}, u32[]{:S(2)}) copy-start(f32[12,32]{1,0:T(8,128)S(1)} %fusion.224) | copy-start | bytes 4612 | tf_op jit(solution)/shard_map/while
  406.3 22.0 %collective-permute-start.1 = (bf16[2,2,128,768]{2,3,1,0:T(8,128)(2,1)}, bf16[2,2,128,768]{2,3,1,0:T(8,128)(2,1)S(1)}, u32[]{:S(2)}, u32[]{:S(2)}) collective-permute-start(bf16[2,2,128,768]{2,3,1,0:T(8,128)(2,1)} %get-tuple-element.1127), channel_id=1, source_target_pairs={{28,0},{0,4},{4,8},{8,12},{12,16},{16,20},{20,24},{24,28},{29,1},{... | collective-permute-start | bytes 2359304 | tf_op jit(solution)/shard_map/while/body/eval_jaxpr/ppermute | solution.py:30
  430.8 21.0 %collective-permute-start.2 = (bf16[2,2,128,768]{2,3,1,0:T(8,128)(2,1)S(1)}, bf16[2,2,128,768]{2,3,1,0:T(8,128)(2,1)S(1)}, u32[]{:S(2)}, u32[]{:S(2)}) collective-permute-start(bf16[2,2,128,768]{2,3,1,0:T(8,128)(2,1)S(1)} %fusion.222), channel_id=1, source_target_pairs={{28,0},{0,4},{4,8},{8,12},{12,16},{16,20},{20,24},{24,28},{29,1},{... | collective-permute-start | bytes 2359304 | tf_op jit(solution)/shard_map/while/body/eval_jaxpr/ppermute | solution.py:30
  432.7 19.1 %copy-start.56 = (f32[12,32]{1,0:T(8,128)}, f32[12,32]{1,0:T(8,128)S(1)}, u32[]{:S(2)}) copy-start(f32[12,32]{1,0:T(8,128)S(1)} %fusion.224) | copy-start | bytes 4612 | tf_op jit(solution)/shard_map/while
  451.8 22.6 %collective-permute-start.1 = (bf16[2,2,128,768]{2,3,1,0:T(8,128)(2,1)}, bf16[2,2,128,768]{2,3,1,0:T(8,128)(2,1)S(1)}, u32[]{:S(2)}, u32[]{:S(2)}) collective-permute-start(bf16[2,2,128,768]{2,3,1,0:T(8,128)(2,1)} %get-tuple-element.1127), channel_id=1, source_target_pairs={{28,0},{0,4},{4,8},{8,12},{12,16},{16,20},{20,24},{24,28},{29,1},{... | collective-permute-start | bytes 2359304 | tf_op jit(solution)/shard_map/while/body/eval_jaxpr/ppermute | solution.py:30
  476.8 19.3 %collective-permute-start.2 = (bf16[2,2,128,768]{2,3,1,0:T(8,128)(2,1)S(1)}, bf16[2,2,128,768]{2,3,1,0:T(8,128)(2,1)S(1)}, u32[]{:S(2)}, u32[]{:S(2)}) collective-permute-start(bf16[2,2,128,768]{2,3,1,0:T(8,128)(2,1)S(1)} %fusion.222), channel_id=1, source_target_pairs={{28,0},{0,4},{4,8},{8,12},{12,16},{16,20},{20,24},{24,28},{29,1},{... | collective-permute-start | bytes 2359304 | tf_op jit(solution)/shard_map/while/body/eval_jaxpr/ppermute | solution.py:30
  478.7 17.4 %copy-start.56 = (f32[12,32]{1,0:T(8,128)}, f32[12,32]{1,0:T(8,128)S(1)}, u32[]{:S(2)}) copy-start(f32[12,32]{1,0:T(8,128)S(1)} %fusion.224) | copy-start | bytes 4612 | tf_op jit(solution)/shard_map/while
  496.1 20.8 %collective-permute-start.1 = (bf16[2,2,128,768]{2,3,1,0:T(8,128)(2,1)}, bf16[2,2,128,768]{2,3,1,0:T(8,128)(2,1)S(1)}, u32[]{:S(2)}, u32[]{:S(2)}) collective-permute-start(bf16[2,2,128,768]{2,3,1,0:T(8,128)(2,1)} %get-tuple-element.1127), channel_id=1, source_target_pairs={{28,0},{0,4},{4,8},{8,12},{12,16},{16,20},{20,24},{24,28},{29,1},{... | collective-permute-start | bytes 2359304 | tf_op jit(solution)/shard_map/while/body/eval_jaxpr/ppermute | solution.py:30
  519.4 17.4 %collective-permute-start.2 = (bf16[2,2,128,768]{2,3,1,0:T(8,128)(2,1)S(1)}, bf16[2,2,128,768]{2,3,1,0:T(8,128)(2,1)S(1)}, u32[]{:S(2)}, u32[]{:S(2)}) collective-permute-start(bf16[2,2,128,768]{2,3,1,0:T(8,128)(2,1)S(1)} %fusion.222), channel_id=1, source_target_pairs={{28,0},{0,4},{4,8},{8,12},{12,16},{16,20},{20,24},{24,28},{29,1},{... | collective-permute-start | bytes 2359304 | tf_op jit(solution)/shard_map/while/body/eval_jaxpr/ppermute | solution.py:30
  521.3 15.6 %copy-start.56 = (f32[12,32]{1,0:T(8,128)}, f32[12,32]{1,0:T(8,128)S(1)}, u32[]{:S(2)}) copy-start(f32[12,32]{1,0:T(8,128)S(1)} %fusion.224) | copy-start | bytes 4612 | tf_op jit(solution)/shard_map/while
  536.9 19.0 %collective-permute-start.1 = (bf16[2,2,128,768]{2,3,1,0:T(8,128)(2,1)}, bf16[2,2,128,768]{2,3,1,0:T(8,128)(2,1)S(1)}, u32[]{:S(2)}, u32[]{:S(2)}) collective-permute-start(bf16[2,2,128,768]{2,3,1,0:T(8,128)(2,1)} %get-tuple-element.1127), channel_id=1, source_target_pairs={{28,0},{0,4},{4,8},{8,12},{12,16},{16,20},{20,24},{24,28},{29,1},{... | collective-permute-start | bytes 2359304 | tf_op jit(solution)/shard_map/while/body/eval_jaxpr/ppermute | solution.py:30
  558.3 14.7 %collective-permute-start.2 = (bf16[2,2,128,768]{2,3,1,0:T(8,128)(2,1)S(1)}, bf16[2,2,128,768]{2,3,1,0:T(8,128)(2,1)S(1)}, u32[]{:S(2)}, u32[]{:S(2)}) collective-permute-start(bf16[2,2,128,768]{2,3,1,0:T(8,128)(2,1)S(1)} %fusion.222), channel_id=1, source_target_pairs={{28,0},{0,4},{4,8},{8,12},{12,16},{16,20},{20,24},{24,28},{29,1},{... | collective-permute-start | bytes 2359304 | tf_op jit(solution)/shard_map/while/body/eval_jaxpr/ppermute | solution.py:30
  560.2 12.9 %copy-start.56 = (f32[12,32]{1,0:T(8,128)}, f32[12,32]{1,0:T(8,128)S(1)}, u32[]{:S(2)}) copy-start(f32[12,32]{1,0:T(8,128)S(1)} %fusion.224) | copy-start | bytes 4612 | tf_op jit(solution)/shard_map/while
  575.7 52.0 %reduce-scatter.11.cloned.1.call-start = ((), (), s32[]{:S(2)}) async-start(), calls=%async_computation.14 | async-start | bytes 1474560 | tf_op jit(solution)/shard_map/reduce_scatter | solution.py:361
  577.3 79.3 %reduce-scatter.7.cloned.1.call-start = ((), (), s32[]{:S(2)}) async-start(), calls=%async_computation.12 | async-start | bytes 1474560 | tf_op jit(solution)/shard_map/reduce_scatter | solution.py:355
  579.4 127.6 %reduce-scatter.17.cloned.1.call-start = ((), (), s32[]{:S(2)}) async-start(), calls=%async_computation.17 | async-start | bytes 5898240 | tf_op jit(solution)/shard_map/reduce_scatter | solution.py:376
  583.2 174.2 %reduce-scatter.15.cloned.1.call-start = ((), (), s32[]{:S(2)}) async-start(), calls=%async_computation.16 | async-start | bytes 5898240 | tf_op jit(solution)/shard_map/reduce_scatter | solution.py:373
  593.0 11.1 %copy-start.52 = (f32[2,128]{1,0:T(2,128)S(1)}, f32[2,128]{1,0:T(2,128)}, u32[]{:S(2)}) copy-start(f32[2,128]{1,0:T(2,128)} %copy-done.51) | copy-start | bytes 3076
  593.0 11.1 %copy-start.3 = (f32[256,768]{1,0:T(8,128)S(1)}, f32[256,768]{1,0:T(8,128)}, u32[]{:S(2)}) copy-start(f32[256,768]{1,0:T(8,128)} %copy-done.2) | copy-start | bytes 2359300
  (87 other events, 136.7 us)
Sparse Core Ops, SparseCore 0:
  9.6 20.2 all-gather.10
  31.5 17.4 all-gather.6
  50.5 17.4 all-gather.8
  69.4 17.4 all-gather.12
  88.4 37.4 all-gather.14
  127.3 37.4 all-gather.16
  268.5 27.3 reduce-scatter.12
  575.8 23.3 reduce-scatter.8
  601.8 25.8 reduce-scatter.10
  630.8 25.7 reduce-scatter.6
  659.1 47.8 reduce-scatter.16
  709.6 47.8 reduce-scatter.14
